TPU v7x, 512 devices: a whole 4x4x16 slice. The times are simulated.
512 devices in a mesh: gx: 32 (over z, y_lo), gy: 16 (over y_hi, x, core).
Axes of the slice: x: 4, y: 4 (y_hi: 2, y_lo: 2; y = y_hi * 2 + y_lo), z: 16, core: 2. Of those that a mesh axis runs over, the one named last changes fastest.
Arguments:
- delta: float32 [4, 512, 256, 128], P(None, 'gx', 'gy'), may hold values from -6 to 6
- alpha: float32 [32, 64, 4, 128], P('gx', 'gy'), may hold values from -6 to 6
- eddy: float32 [512, 256, 128], P('gx', 'gy'), may hold values from 0.02 to 0.2
- courant: float32 [2, 512, 256, 128], P(None, 'gx', 'gy'), may hold values from -0.4 to 0.4
- tile_map: int32 [512, 256], P('gx', 'gy'), may hold values from 0 to 63
- obs_rows: float32 [4096, 3, 128], P(('gx', 'gy')), may hold values from -6 to 6
- gate_beam: int32 [32, 16, 256], P('gx', 'gy'), may hold values from 0 to 255
- gate_index: int32 [32, 16, 256], P('gx', 'gy'), may hold values from 0 to 127
- gate_column: int32 [32, 16, 256], P('gx', 'gy'), may hold values from 0 to 255
- gate_live: int32 [32, 16, 256], P('gx', 'gy'), may hold values 0 or 1
- obs_weight: float32 [32, 16, 256, 4, 128], P('gx', 'gy'), may hold values from -0.25 to 0.25
- obs_precision: float32 [32, 16, 256], P('gx', 'gy'), may hold values from 4 to 64
Outputs:
- grad_delta: float32 [4, 512, 256, 128], P(None, 'gx', 'gy')
- grad_alpha: float32 [32, 64, 4, 128], P('gx', 'gy')
Inputs may be any that keep to these rules, and one draw needn't show every extreme that they name: `gate_beam`: a slot's beam is numbered within its own north-south row of tiles as the east-west index of the beam's owner times 8 plus its place among that owner's beams. `gate_column`: column index within the tile is east-west offset times 16 plus north-south offset.
All inputs are finite; a program needn't handle non-finite values. No bound on the sum of `gate_live` on one device may be relied on, other than what follows from the above.
Results may differ from a plain program's by a relative error of at most 0.00011.
Values sent between devices are 32-bit elements; how exact they have to be, the bound alone decides.
A program may use at most 64 MiB of HBM per device.

v0:
```python
import jax
import jax.numpy as jnp
from jax import lax
from jax.sharding import PartitionSpec as P

STEPS = 3


profile_weight = 0.125
highest = lax.Precision.HIGHEST


def padded_2(block, sides, width):
    for axis, dim in sides:
        count = lax.axis_size(axis)
        forward = [(i, i + 1) for i in range(count - 1)]
        backward = [(target, source) for source, target in forward]
        low = lax.ppermute(
            lax.slice_in_dim(block, block.shape[dim] - width, None, axis=dim), axis, forward
        )
        high = lax.ppermute(lax.slice_in_dim(block, 0, width, axis=dim), axis, backward)
        block = jnp.concatenate([low, block, high], axis=dim)
    return block


def advance(padded, coefs):
    centre = padded[:, 1:-1, 1:-1]
    east_side = padded[:, 2:, 1:-1]
    west_side = padded[:, :-2, 1:-1]
    north_side = padded[:, 1:-1, 2:]
    south_side = padded[:, 1:-1, :-2]
    return (
        centre
        + coefs[0] * (east_side + west_side + north_side + south_side - 4.0 * centre)
        - 0.5 * coefs[1] * (east_side - west_side)
        - 0.5 * coefs[2] * (north_side - south_side)
    )


def trimmed(padded_coefs, margin, rows, columns):
    first = STEPS - margin
    return padded_coefs[:, first : first + rows + 2 * margin, first : first + columns + 2 * margin]


def transpose_step(padded, coefs):
    viscous = coefs[0]
    along_x = coefs[1]
    along_y = coefs[2]
    centre = padded[:, 1:-1, 1:-1]
    result = (1.0 - 4.0 * viscous[1:-1, 1:-1]) * centre
    result = result + (viscous[:-2, 1:-1] - 0.5 * along_x[:-2, 1:-1]) * padded[:, :-2, 1:-1]
    result = result + (viscous[2:, 1:-1] + 0.5 * along_x[2:, 1:-1]) * padded[:, 2:, 1:-1]
    result = result + (viscous[1:-1, :-2] - 0.5 * along_y[1:-1, :-2]) * padded[:, 1:-1, :-2]
    result = result + (viscous[1:-1, 2:] + 0.5 * along_y[1:-1, 2:]) * padded[:, 1:-1, 2:]
    return result


def retreat(adjoint, padded_coefs, rows, columns):
    padded = padded_2(adjoint, (("gx", 1), ("gy", 2)), 1)
    return transpose_step(padded, trimmed(padded_coefs, 1, rows, columns))


def observed_values(obs_rows, beams, gates):
    ngates = obs_rows.shape[2]
    values = []
    for step in range(STEPS):
        gathered = lax.all_gather(obs_rows[:, step, :], "gx", axis=0, tiled=True)
        values.append(gathered.reshape(-1)[beams * ngates + gates])
    return values


def on_device(
    delta,
    alpha,
    eddy,
    courant,
    tile_map,
    obs_rows,
    gate_beam,
    gate_index,
    gate_column,
    gate_live,
    obs_weight,
    obs_precision,
):
    rows, columns, levels = (delta.shape[1], delta.shape[2], delta.shape[3])
    owned_tiles = alpha.shape[1]
    strip_tiles = owned_tiles * lax.axis_size("gy")
    coefs = jnp.concatenate([eddy[None], courant], axis=0)
    padded_coefs = padded_2(coefs, (("gx", 1), ("gy", 2)), STEPS)
    selector = (tile_map.reshape(-1)[:, None] == lax.iota(jnp.int32, strip_tiles)[None, :]).astype(
        jnp.float32
    )
    piece = lax.all_gather(alpha, "gy", axis=1, tiled=True)
    profiles = jnp.dot(selector, piece[0].reshape(piece.shape[1], 4 * levels), precision=highest)
    profiles = jnp.transpose(profiles.reshape(rows, columns, 4, levels), (2, 0, 1, 3))
    state = delta + profile_weight * profiles
    beams = gate_beam[0, 0]
    gates = gate_index[0, 0]
    slots = gate_column[0, 0]
    weights = obs_weight[0, 0]
    scaled = gate_live[0, 0].astype(jnp.float32) * obs_precision[0, 0]
    observed = observed_values(obs_rows, beams, gates)
    states = []
    for step in range(STEPS):
        padded = padded_2(state, (("gx", 1), ("gy", 2)), 1)
        state = advance(padded, trimmed(padded_coefs, 0, rows, columns))
        states.append(state)
    forcings = []
    for step in range(STEPS):
        picked = jnp.take(states[step].reshape(4, rows * columns, levels), slots, axis=1)
        seen = jnp.einsum("cgz,gcz->g", picked, weights, precision=highest)
        misfit = scaled * (seen - observed[step])
        pushed = jax.ops.segment_sum(
            misfit[:, None, None] * weights, slots, num_segments=rows * columns
        )
        forcings.append(jnp.transpose(pushed.reshape(rows, columns, 4, levels), (2, 0, 1, 3)))
    adjoint = forcings[STEPS - 1]
    for step in range(STEPS - 1, -1, -1):
        adjoint = retreat(adjoint, padded_coefs, rows, columns)
        if step > 0:
            adjoint = adjoint + forcings[step - 1]
    flat_adjoint = jnp.transpose(adjoint, (1, 2, 0, 3)).reshape(rows * columns, 4 * levels)
    picked = selector
    sums = lax.psum_scatter(
        lax.dot_general(picked, flat_adjoint, (((0,), (0,)), ((), ())), precision=highest),
        "gy",
        scatter_dimension=0,
        tiled=True,
    )
    grad_alpha = alpha + profile_weight * sums.reshape(1, owned_tiles, 4, levels)
    return (delta + adjoint, grad_alpha)


def solution(mesh):
    return jax.shard_map(
        on_device,
        mesh=mesh,
        in_specs=(
            P(None, "gx", "gy", None),
            P("gx", "gy", None, None),
            P("gx", "gy", None),
            P(None, "gx", "gy", None),
            P("gx", "gy"),
            P(("gx", "gy"), None, None),
            P("gx", "gy", None),
            P("gx", "gy", None),
            P("gx", "gy", None),
            P("gx", "gy", None),
            P("gx", "gy", None, None, None),
            P("gx", "gy", None),
        ),
        out_specs=(P(None, "gx", "gy", None), P("gx", "gy", None, None)),
        check_vma=False,
    )
```

profile of v0, /device:TPU:481, one launch (start us, length us, event | category | flops | bytes accessed | tf_op | source)
XLA Modules:
  0.0 539.3 jit_solution(3159348896849731889)
XLA Ops:
  7.2 25.4 %all_gather.12 = f32[1,64,4,128]{3,2,0,1:T(4,128)S(1)} all-gather(f32[1,4,4,128]{3,2,0,1:T(4,128)} %bitcast.108), channel_id=1, replica_groups=mesh['gx'=32,'gy'=16] {'gy'}, dimensions={1}, use_global_device_ids=true | all-gather | bytes 139264 | tf_op jit(solution)/shard_map/all_gather | solution.py:94
  34.2 2.9 collective-permute-start.4
  37.1 2.5 collective-permute-start.5
  41.6 4.3 collective-permute-start.1
  48.1 3.2 collective-permute-start.6
  51.3 2.4 collective-permute-start.7
  55.1 2.8 collective-permute-start.8
  57.8 2.5 collective-permute-start.9
  60.4 45.8 %all-gather = f32[256,1,128]{2,0,1:T(8,128)S(1)} all-gather(f32[8,1,128]{2,0,1:T(8,128)S(1)} %get-tuple-element.53), channel_id=2, replica_groups=mesh['gx'=32,'gy'=16] {'gx'}, dimensions={0}, use_global_device_ids=true | all-gather | bytes 135168 | tf_op jit(solution)/shard_map/all_gather | solution.py:67
  108.0 16.2 %collective-permute-start.10 = (f32[4,18,1,128]{3,2,0,1:T(1,128)S(1)}, f32[4,18,1,128]{3,2,0,1:T(1,128)S(1)}, u32[]{:S(2)}, u32[]{:S(2)}) collective-permute-start(f32[4,18,1,128]{3,2,0,1:T(1,128)S(1)} %get-tuple-element.19), channel_id=1, source_target_pairs={{1,0},{2,1},{3,2},{4,3},{5,4},{6,5},{7,6},{8,7},{9,8},{10,9},{11,1... | collective-permute-start | bytes 110600 | tf_op jit(solution)/shard_map/ppermute | solution.py:21
  124.2 4.4 collective-permute-start.11
  128.6 45.7 %all-gather.1 = f32[256,1,128]{2,0,1:T(8,128)S(1)} all-gather(f32[8,1,128]{2,0,1:T(8,128)S(1)} %get-tuple-element.54), channel_id=3, replica_groups=mesh['gx'=32,'gy'=16] {'gx'}, dimensions={0}, use_global_device_ids=true | all-gather | bytes 135168 | tf_op jit(solution)/shard_map/all_gather | solution.py:67
  176.4 5.1 collective-permute-start.12
  183.5 47.3 %all-gather.2 = f32[256,1,128]{2,0,1:T(8,128)S(1)} all-gather(f32[8,1,128]{2,0,1:T(8,128)S(1)} %get-tuple-element.52), channel_id=4, replica_groups=mesh['gx'=32,'gy'=16] {'gx'}, dimensions={0}, use_global_device_ids=true | all-gather | bytes 135168 | tf_op jit(solution)/shard_map/all_gather | solution.py:67
  233.9 28.0 %collective-permute-start.14 = (f32[4,18,1,128]{3,2,0,1:T(1,128)S(1)}, f32[4,18,1,128]{3,2,0,1:T(1,128)S(1)}, u32[]{:S(2)}, u32[]{:S(2)}) collective-permute-start(f32[4,18,1,128]{3,2,0,1:T(1,128)S(1)} %get-tuple-element.17), channel_id=1, source_target_pairs={{1,0},{2,1},{3,2},{4,3},{5,4},{6,5},{7,6},{8,7},{9,8},{10,9},{11,1... | collective-permute-start | bytes 110600 | tf_op jit(solution)/shard_map/ppermute | solution.py:21
  261.9 4.5 collective-permute-start.15
  267.3 2.4 collective-permute-start.2
  269.7 2.6 collective-permute-start.3
  275.4 4.4 fusion.33
  281.1 8.3 %scatter_fusion = f32[256,4,128]{2,1,0:T(4,128)S(1)} fusion(f32[256,4,128]{2,1,0:T(4,128)S(1)} %broadcast.96.clone, s32[256]{0:T(256)S(1)} %bitcast.111, f32[256,4,128]{2,1,0:T(4,128)S(1)} %get-tuple-element.29), kind=kCustom, calls=%fused_computation.6 | custom fusion | flops 131072 | bytes 1573888 | tf_op jit(solution)/shard_map/scatter-add | solution.py:114
  289.5 1.9 collective-permute-start.16
  291.4 4.3 collective-permute-start.17
  296.8 4.1 collective-permute-start.18
  303.0 8.3 %scatter_fusion.1 = f32[256,4,128]{2,1,0:T(4,128)S(1)} fusion(f32[256,4,128]{2,1,0:T(4,128)S(1)} %broadcast.96.clone.1, s32[256]{0:T(256)S(1)} %bitcast.112, f32[256,4,128]{2,1,0:T(4,128)S(1)} %get-tuple-element.28), kind=kCustom, calls=%fused_computation.7 | custom fusion | flops 131072 | bytes 1573888 | tf_op jit(solution)/shard_map/scatter-add | solution.py:114
  313.6 4.9 collective-permute-start.21
  319.6 4.5 collective-permute-start.22
  326.1 8.3 %scatter_fusion.2 = f32[256,4,128]{2,1,0:T(4,128)S(1)} fusion(f32[256,4,128]{2,1,0:T(4,128)S(1)} %broadcast.96.clone.2, s32[256]{0:T(256)S(1)} %bitcast.113, f32[256,4,128]{2,1,0:T(4,128)S(1)} %get-tuple-element.27), kind=kCustom, calls=%fused_computation.8 | custom fusion | flops 131072 | bytes 1573888 | tf_op jit(solution)/shard_map/scatter-add | solution.py:114
  334.8 2.1 collective-permute-start.24
  336.8 4.9 collective-permute-start.25
  342.8 4.5 collective-permute-start.26
  349.3 3.3 collective-permute-done.27
  356.9 173.6 %all-reduce.3.cloned.1.call-done = f32[64,512]{1,0:T(8,128)} async-done(((f32[64,512]{1,0:T(8,128)}), f32[64,512]{1,0:T(8,128)}) %all-reduce.3.cloned.1.call-update) | async-done | bytes 131088
  (115 shorter events, 38.7 us)
Async XLA Ops:
  7.2 523.3 %all-reduce.3.cloned.1.call-start = ((), (), s32[]{:S(2)}) async-start(), calls=%async_computation | async-start | bytes 262144
  7.2 25.4 %copy-start.4 = (s32[16,16]{1,0:T(8,128)S(1)}, s32[16,16]{1,0:T(8,128)}, u32[]{:S(2)}) copy-start(s32[16,16]{1,0:T(8,128)} %param.18) | copy-start | bytes 3076
  32.6 7.0 %copy-start.1 = (f32[2,16,16,128]{3,2,1,0:T(8,128)S(1)}, f32[2,16,16,128]{3,2,1,0:T(8,128)}, u32[]{:S(2)}) copy-start(f32[2,16,16,128]{3,2,1,0:T(8,128)} %param.17) | copy-start | bytes 786436
  34.2 13.8 %collective-permute-start.4 = (f32[4,1,16,128]{3,2,0,1:T(8,128)S(1)}, f32[4,1,16,128]{3,2,0,1:T(8,128)S(1)}, u32[]{:S(2)}, u32[]{:S(2)}) collective-permute-start(f32[4,1,16,128]{3,2,0,1:T(8,128)S(1)} %get-tuple-element.39), channel_id=1, source_target_pairs={{16,0},{32,16},{48,32},{64,48},{80,64},{96,80},{112,96},{128,112},... | collective-permute-start | bytes 98312 | tf_op jit(solution)/shard_map/ppermute | solution.py:21
  37.1 10.9 %collective-permute-start.5 = (f32[4,1,16,128]{3,2,0,1:T(8,128)S(1)}, f32[4,1,16,128]{3,2,0,1:T(8,128)S(1)}, u32[]{:S(2)}, u32[]{:S(2)}) collective-permute-start(f32[4,1,16,128]{3,2,0,1:T(8,128)S(1)} %get-tuple-element.38), channel_id=1, source_target_pairs={{0,16},{16,32},{32,48},{48,64},{64,80},{80,96},{96,112},{112,128},... | collective-permute-start | bytes 98312 | tf_op jit(solution)/shard_map/ppermute | solution.py:18
  39.6 226.9 %collective-permute-start = (f32[3,3,16,128]{3,2,1,0:T(8,128)S(1)}, f32[3,3,16,128]{3,2,1,0:T(8,128)S(1)}, u32[]{:S(2)}, u32[]{:S(2)}) collective-permute-start(f32[3,3,16,128]{3,2,1,0:T(8,128)S(1)} %get-tuple-element.44), channel_id=1, source_target_pairs={{0,16},{16,32},{32,48},{48,64},{64,80},{80,96},{96,112},{112,128},... | collective-permute-start | bytes 221192 | tf_op jit(solution)/shard_map/ppermute | solution.py:18
  41.6 224.9 %collective-permute-start.1 = (f32[3,3,16,128]{3,2,1,0:T(8,128)S(1)}, f32[3,3,16,128]{3,2,1,0:T(8,128)S(1)}, u32[]{:S(2)}, u32[]{:S(2)}) collective-permute-start(f32[3,3,16,128]{3,2,1,0:T(8,128)S(1)} %get-tuple-element.45), channel_id=1, source_target_pairs={{16,0},{32,16},{48,32},{64,48},{80,64},{96,80},{112,96},{128,112},... | collective-permute-start | bytes 221192 | tf_op jit(solution)/shard_map/ppermute | solution.py:21
  48.1 5.6 %collective-permute-start.6 = (f32[4,18,1,128]{3,2,0,1:T(1,128)S(1)}, f32[4,18,1,128]{3,2,0,1:T(1,128)S(1)}, u32[]{:S(2)}, u32[]{:S(2)}) collective-permute-start(f32[4,18,1,128]{3,2,0,1:T(1,128)S(1)} %get-tuple-element.21), channel_id=1, source_target_pairs={{1,0},{2,1},{3,2},{4,3},{5,4},{6,5},{7,6},{8,7},{9,8},{10,9},{11,1... | collective-permute-start | bytes 110600 | tf_op jit(solution)/shard_map/ppermute | solution.py:21
  51.3 3.4 collective-permute-start.7
  55.1 52.8 %collective-permute-start.8 = (f32[4,1,16,128]{3,2,0,1:T(8,128)S(1)}, f32[4,1,16,128]{3,2,0,1:T(8,128)S(1)}, u32[]{:S(2)}, u32[]{:S(2)}) collective-permute-start(f32[4,1,16,128]{3,2,0,1:T(8,128)S(1)} %get-tuple-element.37), channel_id=1, source_target_pairs={{16,0},{32,16},{48,32},{64,48},{80,64},{96,80},{112,96},{128,112},... | collective-permute-start | bytes 98312 | tf_op jit(solution)/shard_map/ppermute | solution.py:21
  57.8 50.1 %collective-permute-start.9 = (f32[4,1,16,128]{3,2,0,1:T(8,128)S(1)}, f32[4,1,16,128]{3,2,0,1:T(8,128)S(1)}, u32[]{:S(2)}, u32[]{:S(2)}) collective-permute-start(f32[4,1,16,128]{3,2,0,1:T(8,128)S(1)} %get-tuple-element.36), channel_id=1, source_target_pairs={{0,16},{16,32},{32,48},{48,64},{64,80},{80,96},{96,112},{112,128},... | collective-permute-start | bytes 98312 | tf_op jit(solution)/shard_map/ppermute | solution.py:18
  108.0 68.1 %collective-permute-start.10 = (f32[4,18,1,128]{3,2,0,1:T(1,128)S(1)}, f32[4,18,1,128]{3,2,0,1:T(1,128)S(1)}, u32[]{:S(2)}, u32[]{:S(2)}) collective-permute-start(f32[4,18,1,128]{3,2,0,1:T(1,128)S(1)} %get-tuple-element.19), channel_id=1, source_target_pairs={{1,0},{2,1},{3,2},{4,3},{5,4},{6,5},{7,6},{8,7},{9,8},{10,9},{11,1... | collective-permute-start | bytes 110600 | tf_op jit(solution)/shard_map/ppermute | solution.py:21
  124.2 51.8 %collective-permute-start.11 = (f32[4,18,1,128]{3,2,0,1:T(1,128)S(1)}, f32[4,18,1,128]{3,2,0,1:T(1,128)S(1)}, u32[]{:S(2)}, u32[]{:S(2)}) collective-permute-start(f32[4,18,1,128]{3,2,0,1:T(1,128)S(1)} %get-tuple-element.20), channel_id=1, source_target_pairs={{0,1},{1,2},{2,3},{3,4},{4,5},{5,6},{6,7},{7,8},{8,9},{9,10},{10,1... | collective-permute-start | bytes 110600 | tf_op jit(solution)/shard_map/ppermute | solution.py:18
  176.4 57.4 %collective-permute-start.12 = (f32[4,1,16,128]{3,2,0,1:T(8,128)S(1)}, f32[4,1,16,128]{3,2,0,1:T(8,128)S(1)}, u32[]{:S(2)}, u32[]{:S(2)}) collective-permute-start(f32[4,1,16,128]{3,2,0,1:T(8,128)S(1)} %get-tuple-element.35), channel_id=1, source_target_pairs={{16,0},{32,16},{48,32},{64,48},{80,64},{96,80},{112,96},{128,112},... | collective-permute-start | bytes 98312 | tf_op jit(solution)/shard_map/ppermute | solution.py:21
  181.5 52.3 %collective-permute-start.13 = (f32[4,1,16,128]{3,2,0,1:T(8,128)S(1)}, f32[4,1,16,128]{3,2,0,1:T(8,128)S(1)}, u32[]{:S(2)}, u32[]{:S(2)}) collective-permute-start(f32[4,1,16,128]{3,2,0,1:T(8,128)S(1)} %get-tuple-element.34), channel_id=1, source_target_pairs={{0,16},{16,32},{32,48},{48,64},{64,80},{80,96},{96,112},{112,128},... | collective-permute-start | bytes 98312 | tf_op jit(solution)/shard_map/ppermute | solution.py:18
  233.9 39.7 %collective-permute-start.14 = (f32[4,18,1,128]{3,2,0,1:T(1,128)S(1)}, f32[4,18,1,128]{3,2,0,1:T(1,128)S(1)}, u32[]{:S(2)}, u32[]{:S(2)}) collective-permute-start(f32[4,18,1,128]{3,2,0,1:T(1,128)S(1)} %get-tuple-element.17), channel_id=1, source_target_pairs={{1,0},{2,1},{3,2},{4,3},{5,4},{6,5},{7,6},{8,7},{9,8},{10,9},{11,1... | collective-permute-start | bytes 110600 | tf_op jit(solution)/shard_map/ppermute | solution.py:21
  261.9 11.7 %collective-permute-start.15 = (f32[4,18,1,128]{3,2,0,1:T(1,128)S(1)}, f32[4,18,1,128]{3,2,0,1:T(1,128)S(1)}, u32[]{:S(2)}, u32[]{:S(2)}) collective-permute-start(f32[4,18,1,128]{3,2,0,1:T(1,128)S(1)} %get-tuple-element.18), channel_id=1, source_target_pairs={{0,1},{1,2},{2,3},{3,4},{4,5},{5,6},{6,7},{7,8},{8,9},{9,10},{10,1... | collective-permute-start | bytes 110600 | tf_op jit(solution)/shard_map/ppermute | solution.py:18
  267.3 28.5 %collective-permute-start.2 = (f32[3,22,3,128]{3,2,1,0:T(4,128)}, f32[3,22,3,128]{3,2,1,0:T(4,128)}, u32[]{:S(2)}, u32[]{:S(2)}) collective-permute-start(f32[3,22,3,128]{3,2,1,0:T(4,128)} %get-tuple-element.23), channel_id=1, source_target_pairs={{0,1},{1,2},{2,3},{3,4},{4,5},{5,6},{6,7},{7,8},{8,9},{9,10},{10,1... | collective-permute-start | bytes 304136 | tf_op jit(solution)/shard_map/ppermute | solution.py:18
  269.7 26.1 %collective-permute-start.3 = (f32[3,22,3,128]{3,2,1,0:T(4,128)}, f32[3,22,3,128]{3,2,1,0:T(4,128)}, u32[]{:S(2)}, u32[]{:S(2)}) collective-permute-start(f32[3,22,3,128]{3,2,1,0:T(4,128)} %get-tuple-element.24), channel_id=1, source_target_pairs={{1,0},{2,1},{3,2},{4,3},{5,4},{6,5},{7,6},{8,7},{9,8},{10,9},{11,1... | collective-permute-start | bytes 304136 | tf_op jit(solution)/shard_map/ppermute | solution.py:21
  289.5 7.2 %collective-permute-start.16 = (f32[4,1,16,128]{3,2,1,0:T(8,128)S(1)}, f32[4,1,16,128]{3,2,1,0:T(8,128)S(1)}, u32[]{:S(2)}, u32[]{:S(2)}) collective-permute-start(f32[4,1,16,128]{3,2,1,0:T(8,128)S(1)} %get-tuple-element.32), channel_id=1, source_target_pairs={{0,16},{16,32},{32,48},{48,64},{64,80},{80,96},{96,112},{112,128},... | collective-permute-start | bytes 98312 | tf_op jit(solution)/shard_map/ppermute | solution.py:18
  291.4 5.3 collective-permute-start.17
  296.8 14.5 %collective-permute-start.18 = (f32[4,18,1,128]{3,2,1,0:T(1,128)S(1)}, f32[4,18,1,128]{3,2,1,0:T(1,128)S(1)}, u32[]{:S(2)}, u32[]{:S(2)}) collective-permute-start(f32[4,18,1,128]{3,2,1,0:T(1,128)S(1)} %get-tuple-element.15), channel_id=1, source_target_pairs={{0,1},{1,2},{2,3},{3,4},{4,5},{5,6},{6,7},{7,8},{8,9},{9,10},{10,1... | collective-permute-start | bytes 110600 | tf_op jit(solution)/shard_map/ppermute | solution.py:18
  300.9 10.5 %collective-permute-start.19 = (f32[4,18,1,128]{3,2,1,0:T(1,128)S(1)}, f32[4,18,1,128]{3,2,1,0:T(1,128)S(1)}, u32[]{:S(2)}, u32[]{:S(2)}) collective-permute-start(f32[4,18,1,128]{3,2,1,0:T(1,128)S(1)} %get-tuple-element.16), channel_id=1, source_target_pairs={{1,0},{2,1},{3,2},{4,3},{5,4},{6,5},{7,6},{8,7},{9,8},{10,9},{11,1... | collective-permute-start | bytes 110600 | tf_op jit(solution)/shard_map/ppermute | solution.py:21
  311.7 6.8 %collective-permute-start.20 = (f32[4,1,16,128]{3,2,1,0:T(8,128)S(1)}, f32[4,1,16,128]{3,2,1,0:T(8,128)S(1)}, u32[]{:S(2)}, u32[]{:S(2)}) collective-permute-start(f32[4,1,16,128]{3,2,1,0:T(8,128)S(1)} %get-tuple-element.30), channel_id=1, source_target_pairs={{0,16},{16,32},{32,48},{48,64},{64,80},{80,96},{96,112},{112,128},... | collective-permute-start | bytes 98312 | tf_op jit(solution)/shard_map/ppermute | solution.py:18
  313.6 5.9 %collective-permute-start.21 = (f32[4,1,16,128]{3,2,1,0:T(8,128)S(1)}, f32[4,1,16,128]{3,2,1,0:T(8,128)S(1)}, u32[]{:S(2)}, u32[]{:S(2)}) collective-permute-start(f32[4,1,16,128]{3,2,1,0:T(8,128)S(1)} %get-tuple-element.31), channel_id=1, source_target_pairs={{16,0},{32,16},{48,32},{64,48},{80,64},{96,80},{112,96},{128,112},... | collective-permute-start | bytes 98312 | tf_op jit(solution)/shard_map/ppermute | solution.py:21
  319.6 14.9 %collective-permute-start.22 = (f32[4,18,1,128]{3,2,1,0:T(1,128)S(1)}, f32[4,18,1,128]{3,2,1,0:T(1,128)S(1)}, u32[]{:S(2)}, u32[]{:S(2)}) collective-permute-start(f32[4,18,1,128]{3,2,1,0:T(1,128)S(1)} %get-tuple-element.13), channel_id=1, source_target_pairs={{0,1},{1,2},{2,3},{3,4},{4,5},{5,6},{6,7},{7,8},{8,9},{9,10},{10,1... | collective-permute-start | bytes 110600 | tf_op jit(solution)/shard_map/ppermute | solution.py:18
  324.1 10.4 %collective-permute-start.23 = (f32[4,18,1,128]{3,2,1,0:T(1,128)S(1)}, f32[4,18,1,128]{3,2,1,0:T(1,128)S(1)}, u32[]{:S(2)}, u32[]{:S(2)}) collective-permute-start(f32[4,18,1,128]{3,2,1,0:T(1,128)S(1)} %get-tuple-element.14), channel_id=1, source_target_pairs={{1,0},{2,1},{3,2},{4,3},{5,4},{6,5},{7,6},{8,7},{9,8},{10,9},{11,1... | collective-permute-start | bytes 110600 | tf_op jit(solution)/shard_map/ppermute | solution.py:21
  334.7 17.8 %copy-start.3 = (f32[4,16,16,128]{3,2,1,0:T(8,128)S(1)}, f32[4,16,16,128]{3,2,1,0:T(8,128)}, u32[]{:S(2)}) copy-start(f32[4,16,16,128]{3,2,1,0:T(8,128)} %param.14) | copy-start | bytes 1572868
  334.8 6.9 %collective-permute-start.24 = (f32[4,1,16,128]{3,2,1,0:T(8,128)S(1)}, f32[4,1,16,128]{3,2,1,0:T(8,128)S(1)}, u32[]{:S(2)}, u32[]{:S(2)}) collective-permute-start(f32[4,1,16,128]{3,2,1,0:T(8,128)S(1)} %get-tuple-element.25), channel_id=1, source_target_pairs={{0,16},{16,32},{32,48},{48,64},{64,80},{80,96},{96,112},{112,128},... | collective-permute-start | bytes 98312 | tf_op jit(solution)/shard_map/ppermute | solution.py:18
  336.8 5.9 %collective-permute-start.25 = (f32[4,1,16,128]{3,2,1,0:T(8,128)S(1)}, f32[4,1,16,128]{3,2,1,0:T(8,128)S(1)}, u32[]{:S(2)}, u32[]{:S(2)}) collective-permute-start(f32[4,1,16,128]{3,2,1,0:T(8,128)S(1)} %get-tuple-element.26), channel_id=1, source_target_pairs={{16,0},{32,16},{48,32},{64,48},{80,64},{96,80},{112,96},{128,112},... | collective-permute-start | bytes 98312 | tf_op jit(solution)/shard_map/ppermute | solution.py:21
  342.8 6.5 %collective-permute-start.26 = (f32[4,18,1,128]{3,2,1,0:T(1,128)S(1)}, f32[4,18,1,128]{3,2,1,0:T(1,128)S(1)}, u32[]{:S(2)}, u32[]{:S(2)}) collective-permute-start(f32[4,18,1,128]{3,2,1,0:T(1,128)S(1)} %get-tuple-element.11), channel_id=1, source_target_pairs={{0,1},{1,2},{2,3},{3,4},{4,5},{5,6},{6,7},{7,8},{8,9},{9,10},{10,1... | collective-permute-start | bytes 110600 | tf_op jit(solution)/shard_map/ppermute | solution.py:18
  347.3 5.3 collective-permute-start.27
  (9 other events, 11.4 us)
Sparse Core Ops, SparseCore 0:
  355.1 175.3 all-reduce.2
where the time goes:
time: 547 us; the launch traced here: 539 us
  waiting for transfers between devices  180 us (33%)
  blocking collectives  164 us (30%)
  starting transfers between devices  126 us (23%)
  other arithmetic  36.9 us (7%)
  between operations  15.5 us (3%)
  local copies, waits for them, and re-layouts  14.1 us (3%)
    unnamed x2, waiting for transfers between devices  174 us
    all_gather x3, blocking collectives, observed_values(): gathered = lax.all_gather(obs_rows[:, step, :], 'gx', axis=0, tiled=True)  139 us
    ppermute x14, starting transfers between devices, padded_2(): lax.ppermute(lax.slice_in_dim(block, 0, width, axis=dim), axis, backward)  84.7 us
    ppermute x14, starting transfers between devices, padded_2(): lax.ppermute(lax.slice_in_dim(block, block.shape[dim] - width, None, axis...  41.5 us
    all_gather x1, blocking collectives, on_device(): piece = lax.all_gather(alpha, 'gy', axis=1, tiled=True)  25.4 us
    scatter-add x3, other arithmetic, on_device(): jax.ops.segment_sum(misfit[:, None, None] * weights, slots, num_segments=...  25 us
  transfers between devices with their start and end apart: 29, of which 6 were waited for; matrix products, arithmetic and copies ran while one was open for 8% of the time, Pallas kernels for 0%

commit v1 on v0

v1 whole, which is shorter than its diff:
```python
import jax
import jax.numpy as jnp
from jax import lax
from jax.experimental import pallas as pl
from jax.experimental.pallas import tpu as pltpu
from jax.sharding import PartitionSpec as P

STEPS = 3
MESH = pl.DeviceIdType.MESH
f32 = jnp.float32
bf16 = jnp.bfloat16

X0, X1, XB = 4, 20, 24
Y0, Y1, YB = 8, 24, 32

DIRS = [(1, 0), (-1, 0), (0, 1), (0, -1), (1, 1), (1, -1), (-1, 1), (-1, -1)]


def inner_part(sign, lo, hi, width):
    if sign > 0:
        return pl.ds(hi - width, width)
    if sign < 0:
        return pl.ds(lo, width)
    return pl.ds(lo, hi - lo)


def outer_part(sign, lo, hi, width):
    if sign > 0:
        return pl.ds(hi, width)
    if sign < 0:
        return pl.ds(lo - width, width)
    return pl.ds(lo, hi - lo)


def split(value):
    high = value.astype(bf16)
    low = (value - high.astype(f32)).astype(bf16)
    return high, low


def dot(a, b):
    return jnp.dot(a, b, preferred_element_type=f32)


def kernel(
    delta_h, alpha_h, eddy_h, courant_h, tmap_h, obs_h, beam_h, gidx_h, gcol_h, live_h, w_h, prec_h,
    out_d, out_a,
    dl, cf, k5, v0, v1, v2, v3, a1, a2, a3, wv, wc, tm, ov, ob, gbeam, ggate, gcol, glive, gprec,
    al, sums, rsums, rx, ry, rc,
    oh, oht, obh, sel, selt, gmask, scl,
    lsem, asend, arecv, osend, orecv, ysend, yrecv, csend, crecv, hsend, hrecv, psend, precv, ssend, srecv,
):
    nx = lax.axis_size("gx")
    ny = lax.axis_size("gy")
    nz = nx // 2
    ix = lax.axis_index("gx")
    iy = lax.axis_index("gy")
    iz = ix // 2
    il = ix % 2

    local = [
        pltpu.make_async_copy(alpha_h, al.at[iy], lsem.at[0]),
        pltpu.make_async_copy(obs_h, ov, lsem.at[1]),
        pltpu.make_async_copy(eddy_h, cf.at[0, X0:X1, Y0:Y1], lsem.at[2]),
        pltpu.make_async_copy(courant_h, cf.at[pl.ds(1, 2), X0:X1, Y0:Y1], lsem.at[3]),
        pltpu.make_async_copy(tmap_h, tm, lsem.at[4]),
        pltpu.make_async_copy(beam_h, gbeam, lsem.at[5]),
        pltpu.make_async_copy(gidx_h, ggate, lsem.at[6]),
        pltpu.make_async_copy(gcol_h, gcol, lsem.at[7]),
        pltpu.make_async_copy(live_h, glive, lsem.at[8]),
        pltpu.make_async_copy(prec_h, gprec, lsem.at[9]),
        pltpu.make_async_copy(delta_h, dl, lsem.at[10]),
        pltpu.make_async_copy(w_h, wv, lsem.at[11]),
    ]
    for copy in local:
        copy.start()

    def clear_frame(ref, count):
        low = jnp.zeros((count, X0, YB, 128), f32)
        ref[:, 0:X0] = low
        ref[:, X1:XB] = low
        side = jnp.zeros((count, X1 - X0, Y0, 128), f32)
        ref[:, X0:X1, 0:Y0] = side
        ref[:, X0:X1, Y1:YB] = side

    clear_frame(v0, 4)
    clear_frame(cf, 3)
    rx[...] = jnp.zeros_like(rx)
    ry[...] = jnp.zeros_like(ry)
    rc[...] = jnp.zeros_like(rc)

    def there(d):
        dx, dy = DIRS[d]
        ok = None
        for sign, at, count in ((dx, ix, nx), (dy, iy, ny)):
            if sign > 0:
                cond = at < count - 1
            elif sign < 0:
                cond = at > 0
            else:
                continue
            ok = cond if ok is None else jnp.logical_and(ok, cond)
        return ok

    def peer(d):
        dx, dy = DIRS[d]
        return {"gx": ix + dx, "gy": iy + dy}

    barrier = pltpu.get_barrier_semaphore()

    def greet(d, carry):
        pl.semaphore_signal(
            barrier, inc=1, device_id={"gx": ix, "gy": (iy + d) % ny}, device_id_type=MESH
        )
        return carry

    lax.fori_loop(1, ny, greet, 0)

    def greet_z(d, carry):
        pl.semaphore_signal(
            barrier, inc=1, device_id={"gx": ((iz + d) % nz) * 2 + il, "gy": iy}, device_id_type=MESH
        )
        return carry

    lax.fori_loop(1, nz, greet_z, 0)
    expected = (ny - 1) + (nz - 1)
    for d in (0, 1, 4, 5, 6, 7):
        ok = there(d)

        @pl.when(ok)
        def _():
            pl.semaphore_signal(barrier, inc=1, device_id=peer(d), device_id_type=MESH)

        expected = expected + jnp.where(ok, 1, 0)

    local[0].wait()
    local[1].wait()
    for step in range(STEPS):
        ob[il, step, iz] = ov[:, step, :]
    pl.semaphore_wait(barrier, expected)

    def alpha_copy(d):
        return pltpu.make_async_remote_copy(
            src_ref=al.at[iy],
            dst_ref=al.at[iy],
            send_sem=asend.at[d],
            recv_sem=arecv.at[d],
            device_id={"gx": ix, "gy": (iy + d) % ny},
            device_id_type=MESH,
        )

    def alpha_start(d, carry):
        alpha_copy(d).start()
        return carry

    lax.fori_loop(1, ny, alpha_start, 0)

    def obs_copy(d):
        return pltpu.make_async_remote_copy(
            src_ref=ob.at[il, :, iz],
            dst_ref=ob.at[il, :, iz],
            send_sem=osend.at[d],
            recv_sem=orecv.at[d],
            device_id={"gx": ((iz + d) % nz) * 2 + il, "gy": iy},
            device_id_type=MESH,
        )

    def obs_start(d, carry):
        obs_copy(d).start()
        return carry

    lax.fori_loop(1, nz, obs_start, 0)

    def halo_copy(ref, d, width, sends, receives):
        dx, dy = DIRS[d]
        if dx != 0 and dy != 0:
            width = width - 1
        return pltpu.make_async_remote_copy(
            src_ref=ref.at[:, inner_part(dx, X0, X1, width), inner_part(dy, Y0, Y1, width)],
            dst_ref=ref.at[:, outer_part(-dx, X0, X1, width), outer_part(-dy, Y0, Y1, width)],
            send_sem=sends.at[d],
            recv_sem=receives.at[d],
            device_id=peer(d),
            device_id_type=MESH,
        )

    def each(make, act, back):
        for d in range(8):
            dx, dy = DIRS[d]
            here = DIRS.index((-dx, -dy)) if back else d

            @pl.when(there(here))
            def _():
                act(make(d))

    def start(copy):
        copy.start()

    def wait_send(copy):
        copy.wait_send()

    def wait_recv(copy):
        copy.wait_recv()

    def coef_copy(d):
        return halo_copy(cf, d, 2, csend, crecv)

    local[2].wait()
    local[3].wait()
    each(coef_copy, start, False)

    for copy in local[4:10]:
        copy.wait()
    lane = lax.broadcasted_iota(jnp.int32, (256, 128), 1).astype(f32)
    row = lax.broadcasted_iota(jnp.int32, (256, 128), 0)

    def spread(values):
        return jnp.broadcast_to(values, (128, 256)).T

    def hot(values):
        return jnp.concatenate(
            [jnp.where(values == lane, 1.0, 0.0), jnp.where(values == lane + 128.0, 1.0, 0.0)], axis=1
        ).astype(bf16)

    of_row = jnp.where(
        row // 16 == lax.broadcasted_iota(jnp.int32, (256, 128), 1), 1.0, 0.0
    ).astype(bf16)
    of_place = (row % 16) == lax.broadcasted_iota(jnp.int32, (256, 128), 1)
    tiles = jnp.zeros((128, 128), f32)
    tiles = jnp.concatenate(
        [
            jnp.concatenate([tm[...].astype(f32), jnp.zeros((16, 112), f32)], axis=1),
            jnp.zeros((112, 128), f32),
        ],
        axis=0,
    ).astype(bf16)
    picked = jnp.where(of_place, dot(of_row, tiles), 0.0).astype(bf16)
    tile_at = dot(picked, jnp.ones((128, 128), bf16))
    for c in range(4):
        sel[c * 256 : (c + 1) * 256] = hot(tile_at * 4.0 + float(c))

    def alpha_wait(d, carry):
        alpha_copy(d).wait_recv()
        return carry

    local[10].wait()
    lax.fori_loop(1, ny, alpha_wait, 0)
    high, low = split(al[...].reshape(256, 128))
    both = jnp.concatenate([high, low], axis=1)
    for c in range(4):
        product = dot(sel[c * 256 : (c + 1) * 256], both)
        profile = (product[:, :128] + product[:, 128:]).reshape(16, 16, 128)
        v0[c, X0:X1, Y0:Y1] = dl[c] + 0.125 * profile

    def state_copy(d):
        return halo_copy(v0, d, 3, hsend, hrecv)

    each(state_copy, start, False)

    slot_column = gcol[0].astype(f32)
    oh[...] = hot(spread(slot_column))
    up = lax.broadcasted_iota(jnp.int32, (256, 256), 0).astype(f32)
    oht[...] = jnp.where(up == slot_column, 1.0, 0.0).astype(bf16)
    beams = gbeam[0]
    place = ((beams // 8) % 2) * 128 + (beams // 16) * 8 + beams % 8
    obh[...] = hot(spread(place.astype(f32)))
    gmask[...] = jnp.where(spread(ggate[0].astype(f32)) == lane, 1.0, 0.0)
    scl[...] = spread(glive[0].astype(f32) * gprec[0])
    tile_row = tile_at.T[0:1]
    for c in range(4):
        selt[:, c * 256 : (c + 1) * 256] = jnp.where(up == tile_row * 4.0 + float(c), 1.0, 0.0).astype(bf16)
    local[11].wait()
    for c in range(4):
        wc[c] = wv[:, c, :]
    clear_frame(a1, 4)
    clear_frame(a2, 4)
    clear_frame(a3, 4)

    each(coef_copy, wait_recv, True)

    def derive(x, carry):
        e = cf[0, x]
        half_x = 0.5 * cf[1, x]
        half_y = 0.5 * cf[2, x]
        k5[0, x] = 1.0 - 4.0 * e
        k5[1, x] = e - half_x
        k5[2, x] = e + half_x
        k5[3, x] = e - half_y
        k5[4, x] = e + half_y
        return carry

    lax.fori_loop(0, XB, derive, 0)

    def obs_wait(d, carry):
        obs_copy(d).wait_recv()
        return carry

    lax.fori_loop(1, nz, obs_wait, 0)
    relay = pltpu.make_async_remote_copy(
        src_ref=ob.at[il],
        dst_ref=ob.at[il],
        send_sem=ysend,
        recv_sem=yrecv.at[il],
        device_id={"gx": iz * 2 + (1 - il), "gy": iy},
        device_id_type=MESH,
    )
    relay.start()
    incoming = pltpu.make_async_remote_copy(
        src_ref=ob.at[1 - il],
        dst_ref=ob.at[1 - il],
        send_sem=ysend,
        recv_sem=yrecv.at[1 - il],
        device_id={"gx": iz * 2 + (1 - il), "gy": iy},
        device_id_type=MESH,
    )

    each(state_copy, wait_recv, True)

    def forward(src, dst, margin):
        y0, rows = (Y0, 16) if margin == 0 else (4, 24)

        def body(x, carry):
            mid = pl.ds(y0, rows)
            dst[:, x, mid] = (
                k5[0, x, mid] * src[:, x, mid]
                + k5[1, x, mid] * src[:, x + 1, mid]
                + k5[2, x, mid] * src[:, x - 1, mid]
                + k5[3, x, mid] * src[:, x, pl.ds(y0 + 1, rows)]
                + k5[4, x, mid] * src[:, x, pl.ds(y0 - 1, rows)]
            )
            return carry

        lax.fori_loop(X0 - margin, X1 + margin, body, 0)

    def backward(src, dst, margin, extra):
        y0, rows = 4, 24

        def body(x, carry):
            mid = pl.ds(y0, rows)
            below = pl.ds(y0 - 1, rows)
            above = pl.ds(y0 + 1, rows)
            dst[:, x, mid] = (
                k5[0, x, mid] * src[:, x, mid]
                + k5[1, x - 1, mid] * src[:, x - 1, mid]
                + k5[2, x + 1, mid] * src[:, x + 1, mid]
                + k5[3, x, below] * src[:, x, below]
                + k5[4, x, above] * src[:, x, above]
            )
            return carry

        lax.fori_loop(X0 - margin, X1 + margin, body, 0)
        if extra is not None:
            for c in range(4):
                dst[c, X0:X1, Y0:Y1] += extra[c]

    def looked(state):
        parts = [split(state[c, X0:X1, Y0:Y1].reshape(256, 128)) for c in range(4)]
        product = dot(oh[...], jnp.concatenate([h for h, _ in parts] + [l for _, l in parts], axis=1))
        total = None
        for c in range(4):
            term = (product[:, c * 128 : (c + 1) * 128] + product[:, 512 + c * 128 : 640 + c * 128]) * wc[c]
            total = term if total is None else total + term
        return total

    clear_frame(v1, 4)
    clear_frame(v2, 4)
    forward(v0, v1, 2)
    seen = [looked(v1)]
    forward(v1, v2, 1)
    seen.append(looked(v2))
    forward(v2, v3, 0)
    seen.append(looked(v3))

    incoming.wait_recv()
    forcings = []
    for step in range(STEPS):
        high, low = split(ob[:, step].reshape(256, 128))
        product = dot(obh[...], jnp.concatenate([high, low], axis=1))
        observed = (product[:, :128] + product[:, 128:]) * gmask[...]
        misfit = scl[...] * jnp.sum(seen[step] - observed, axis=1, keepdims=True)
        parts = [split(misfit * wc[c]) for c in range(4)]
        product = dot(oht[...], jnp.concatenate([h for h, _ in parts] + [l for _, l in parts], axis=1))
        forcings.append(
            [
                (product[:, c * 128 : (c + 1) * 128] + product[:, 512 + c * 128 : 640 + c * 128]).reshape(16, 16, 128)
                for c in range(4)
            ]
        )
    for c in range(4):
        a3[c, X0:X1, Y0:Y1] = forcings[2][c]
    backward(a3, a2, 1, forcings[1])
    backward(a2, a1, 2, forcings[0])
    backward(a1, v1, 3, None)

    def push_copy(d):
        dx, dy = DIRS[d]
        width = 2 if dx != 0 and dy != 0 else 3
        src = v1.at[:, outer_part(dx, X0, X1, width), outer_part(dy, Y0, Y1, width)]
        at_y = inner_part(-dy, 0, 16, width)
        if dy == 0:
            dst = rx.at[:, inner_part(-dx, 0, 6, width)]
        elif dx == 0:
            dst = ry.at[:, :, at_y]
        else:
            dst = rc.at[:, inner_part(-dx, 0, 4, width), at_y]
        return pltpu.make_async_remote_copy(
            src_ref=src,
            dst_ref=dst,
            send_sem=psend.at[d],
            recv_sem=precv.at[d],
            device_id=peer(d),
            device_id_type=MESH,
        )

    each(push_copy, start, False)
    each(push_copy, wait_recv, True)
    total = None
    for c in range(4):
        v3[c, X0:X1, Y0:Y1] = v1[c, X0:X1, Y0:Y1] + ry[c]
        v3[c, X0 : X0 + 3, Y0:Y1] += rx[c, 0:3]
        v3[c, X1 - 3 : X1, Y0:Y1] += rx[c, 3:6]
        v3[c, X0 : X0 + 2, Y0:Y1] += rc[c, 0:2]
        v3[c, X1 - 2 : X1, Y0:Y1] += rc[c, 2:4]
        high, low = split(v3[c, X0:X1, Y0:Y1].reshape(256, 128))
        product = dot(selt[:, c * 256 : (c + 1) * 256], jnp.concatenate([high, low], axis=1))
        term = product[:, :128] + product[:, 128:]
        total = term if total is None else total + term
    sums[...] = total.reshape(16, 16, 128)

    def sums_copy(d):
        target = (iy + d) % ny
        return pltpu.make_async_remote_copy(
            src_ref=sums.at[target],
            dst_ref=rsums.at[d],
            send_sem=ssend.at[d],
            recv_sem=srecv.at[d],
            device_id={"gx": ix, "gy": target},
            device_id_type=MESH,
        )

    def sums_start(d, carry):
        sums_copy(d).start()
        return carry

    lax.fori_loop(1, ny, sums_start, 0)
    rsums[0] = sums[iy]
    for c in range(4):
        out_d[c] = dl[c] + v3[c, X0:X1, Y0:Y1]

    def finish(d, carry):
        sums_copy(d).wait_recv()
        return carry

    lax.fori_loop(1, ny, finish, 0)
    out_a[...] = al[iy] + 0.125 * jnp.sum(rsums[...], axis=0)

    def sent(d, carry):
        alpha_copy(d).wait_send()
        sums_copy(d).wait_send()
        return carry

    lax.fori_loop(1, ny, sent, 0)

    def sent_z(d, carry):
        obs_copy(d).wait_send()
        return carry

    lax.fori_loop(1, nz, sent_z, 0)
    relay.wait_send()
    each(coef_copy, wait_send, False)
    each(state_copy, wait_send, False)
    each(push_copy, wait_send, False)


def on_device(
    delta, alpha, eddy, courant, tile_map, obs_rows,
    gate_beam, gate_index, gate_column, gate_live, obs_weight, obs_precision,
):
    dma = pltpu.SemaphoreType.DMA
    vm = pltpu.VMEM
    frame = vm((4, XB, YB, 128), f32)
    slots = vm((1, 256), jnp.int32)
    anywhere = pl.BlockSpec(memory_space=pl.ANY)
    inside = pl.BlockSpec(memory_space=pltpu.VMEM)
    row = (1, 256)
    adjoint, grad_alpha = pl.pallas_call(
        kernel,
        out_shape=(
            jax.ShapeDtypeStruct((4, 16, 16, 128), f32),
            jax.ShapeDtypeStruct((16, 128), f32),
        ),
        in_specs=[anywhere] * 12,
        out_specs=(inside, inside),
        scratch_shapes=[
            vm((4, 16, 16, 128), f32),
            vm((3, XB, YB, 128), f32),
            vm((5, XB, YB, 128), f32),
            frame, frame, frame, frame,
            frame, frame, frame,
            vm((256, 4, 128), f32),
            vm((4, 256, 128), f32),
            vm((16, 16), jnp.int32),
            vm((8, 3, 128), f32),
            vm((2, 3, 16, 8, 128), f32),
            slots, slots, slots, slots,
            vm((1, 256), f32),
            vm((16, 16, 128), f32),
            vm((16, 16, 128), f32),
            vm((16, 16, 128), f32),
            vm((4, 6, 16, 128), f32),
            vm((4, 16, 16, 128), f32),
            vm((4, 4, 16, 128), f32),
            vm((256, 256), bf16),
            vm((256, 256), bf16),
            vm((256, 256), bf16),
            vm((1024, 256), bf16),
            vm((256, 1024), bf16),
            vm((256, 128), f32),
            vm((256, 128), f32),
            dma((12,)),
            dma((16,)), dma((16,)),
            dma((16,)), dma((16,)),
            dma, dma((2,)),
            dma((8,)), dma((8,)),
            dma((8,)), dma((8,)),
            dma((8,)), dma((8,)),
            dma((16,)), dma((16,)),
        ],
        compiler_params=pltpu.CompilerParams(
            collective_id=0, has_side_effects=True, vmem_limit_bytes=60 * 1024 * 1024
        ),
    )(
        delta,
        alpha.reshape(16, 128),
        eddy,
        courant,
        tile_map,
        obs_rows,
        gate_beam.reshape(row),
        gate_index.reshape(row),
        gate_column.reshape(row),
        gate_live.reshape(row),
        obs_weight.reshape(256, 4, 128),
        obs_precision.reshape(row),
    )
    return adjoint, grad_alpha.reshape(1, 4, 4, 128)


def solution(mesh):
    return jax.shard_map(
        on_device,
        mesh=mesh,
        in_specs=(
            P(None, "gx", "gy", None),
            P("gx", "gy", None, None),
            P("gx", "gy", None),
            P(None, "gx", "gy", None),
            P("gx", "gy"),
            P(("gx", "gy"), None, None),
            P("gx", "gy", None),
            P("gx", "gy", None),
            P("gx", "gy", None),
            P("gx", "gy", None),
            P("gx", "gy", None, None, None),
            P("gx", "gy", None),
        ),
        out_specs=(P(None, "gx", "gy", None), P("gx", "gy", None, None)),
        check_vma=False,
    )
```

time: 547 us -> 59.1 us (0.11)
  the two profiles are of different devices: /device:TPU:481 before, /device:TPU:9 now
where the time goes in v1:
time: 59.1 us; the launch traced here: 58.9 us
  Pallas kernels  54.4 us (92%)
  local copies, waits for them, and re-layouts  3.79 us (6%)
  between operations  0.66 us (1%)
    pallas_call x1, Pallas kernels, on_device(): pl.pallas_call(kernel, out_shape=(jax.ShapeDtypeStruct((4, 16, 16, 128),...  54.4 us
    unnamed x7, local copies, waits for them, and re-layouts  3.79 us

profile of v1, /device:TPU:9, one launch (start us, length us, event | category | flops | bytes accessed | tf_op | source)
XLA Modules:
  0.0 58.9 jit_solution(1984508512367556319)
XLA Ops:
  0.6 0.0 copy-start
  0.6 0.7 %copy-done = f32[8,3,128]{2,0,1:T(8,128)S(1)} copy-done((f32[8,3,128]{2,0,1:T(8,128)S(1)}, f32[8,3,128]{2,0,1:T(8,128)}, u32[]{:S(2)}) %copy-start) | copy-done | bytes 12312
  1.3 0.6 %copy.14.obs_h = f32[8,3,128]{2,1,0:T(4,128)} copy(f32[8,3,128]{2,0,1:T(8,128)S(1)} %copy-done) | data formatting | bytes 24576 | tf_op args[5]
  1.9 54.4 %shard_map.131 = (f32[4,16,16,128]{3,2,1,0:T(8,128)}, f32[16,128]{1,0:T(8,128)}) custom-call(f32[4,16,16,128]{3,2,1,0:T(8,128)} %delta_h.1, f32[16,128]{1,0:T(8,128)} %bitcast.9, f32[16,16,128]{2,1,0:T(8,128)} %eddy_h.1, f32[2,16,16,128]{3,2,1,0:T(8,128)} %courant_h.1, s32[16,16]{1,0:T(8,128)} %tmap_h.1, f32[8,3,128]{2,1,0:T(4,128)} %copy.14.obs_h, ...), custom_call_target="tpu_custom_call" | custom-call | tf_op jit(solution)/shard_map/pallas_call | solution.py:486
  56.4 0.0 copy-start.1
  56.4 1.9 %copy.17 = f32[4,16,16,128]{3,2,1,0:T(8,128)} copy(f32[4,16,16,128]{3,2,1,0:T(8,128)} %get-tuple-element.8) | data formatting | bytes 1048576
  58.3 0.0 copy-done.1
  58.3 0.6 %copy.18 = f32[1,4,4,128]{3,2,1,0:T(4,128)} copy(f32[1,4,4,128]{3,2,1,0:T(4,128)S(1)} %bitcast.10) | data formatting | bytes 16384
Async XLA Ops:
  0.6 0.7 %copy-start = (f32[8,3,128]{2,0,1:T(8,128)S(1)}, f32[8,3,128]{2,0,1:T(8,128)}, u32[]{:S(2)}) copy-start(f32[8,3,128]{2,0,1:T(8,128)} %param.17) | copy-start | bytes 36868
  56.4 1.9 %copy-start.1 = (f32[16,128]{1,0:T(8,128)S(1)}, f32[16,128]{1,0:T(8,128)}, u32[]{:S(2)}) copy-start(f32[16,128]{1,0:T(8,128)} %get-tuple-element.5) | copy-start | bytes 24580

commit v2 on v1

v2 whole, which is shorter than its diff:
```python
import jax
import jax.numpy as jnp
from jax import lax
from jax.experimental import pallas as pl
from jax.experimental.pallas import tpu as pltpu
from jax.sharding import PartitionSpec as P

STEPS = 3
MESH = pl.DeviceIdType.MESH
f32 = jnp.float32
bf16 = jnp.bfloat16

X0, X1, XB = 4, 20, 24
Y0, Y1, YB = 8, 24, 32

DIRS = [(1, 0), (-1, 0), (0, 1), (0, -1), (1, 1), (1, -1), (-1, 1), (-1, -1)]


def inner_part(sign, lo, hi, width):
    if sign > 0:
        return pl.ds(hi - width, width)
    if sign < 0:
        return pl.ds(lo, width)
    return pl.ds(lo, hi - lo)


def outer_part(sign, lo, hi, width):
    if sign > 0:
        return pl.ds(hi, width)
    if sign < 0:
        return pl.ds(lo - width, width)
    return pl.ds(lo, hi - lo)


def split(value):
    high = value.astype(bf16)
    low = (value - high.astype(f32)).astype(bf16)
    return high, low


def dot(a, b):
    return jnp.dot(a, b, preferred_element_type=f32)


def kernel(
    delta_h, alpha_h, eddy_h, courant_h, tmap_h, obs_h, beam_h, gidx_h, gcol_h, live_h, w_h, prec_h,
    out_d, out_a,
    dl, cf, k5, v0, v1, v2, v3, a1, a2, a3, wv, wc, w2, tm, ob, qi, vo, vi, gcol, glive, gprec,
    al, sums, rsums, rx, ry, rc,
    oh, sel, selt,
    lsem, asend, arecv, osend, orecv, qsend, qrecv, wsend, wrecv,
    csend, crecv, hsend, hrecv, psend, precv, ssend, srecv,
):
    nx = lax.axis_size("gx")
    ny = lax.axis_size("gy")
    nq = nx // 4
    ix = lax.axis_index("gx")
    iy = lax.axis_index("gy")
    iq = ix // 4
    im = ix % 4

    def there(d):
        dx, dy = DIRS[d]
        ok = None
        for sign, at, count in ((dx, ix, nx), (dy, iy, ny)):
            if sign > 0:
                cond = at < count - 1
            elif sign < 0:
                cond = at > 0
            else:
                continue
            ok = cond if ok is None else jnp.logical_and(ok, cond)
        return ok

    def peer(d):
        dx, dy = DIRS[d]
        return {"gx": ix + dx, "gy": iy + dy}

    barrier = pltpu.get_barrier_semaphore()

    def greet(gx, gy):
        pl.semaphore_signal(barrier, inc=1, device_id={"gx": gx, "gy": gy}, device_id_type=MESH)

    for t in range(16):

        @pl.when(t != iy)
        def _():
            greet(ix, t)

    expected = (ny - 1) + 3 + iq
    for d in (0, 1, 4, 5, 6, 7):
        ok = there(d)

        @pl.when(ok)
        def _():
            greet(ix + DIRS[d][0], iy + DIRS[d][1])

        expected = expected + jnp.where(ok, 1, 0)
    for m in range(4):

        @pl.when(m != im)
        def _():
            greet(iq * 4 + m, iy)

    for q in range(1, 8):

        @pl.when(q > iq)
        def _():
            greet(q * 4 + im, iy)

    local = [
        pltpu.make_async_copy(eddy_h, cf.at[0, X0:X1, Y0:Y1], lsem.at[0]),
        pltpu.make_async_copy(courant_h, cf.at[pl.ds(1, 2), X0:X1, Y0:Y1], lsem.at[1]),
        pltpu.make_async_copy(beam_h, qi.at[im, pl.ds(0, 1)], lsem.at[2]),
        pltpu.make_async_copy(gidx_h, qi.at[im, pl.ds(1, 1)], lsem.at[3]),
        pltpu.make_async_copy(tmap_h, tm, lsem.at[4]),
        pltpu.make_async_copy(alpha_h, al.at[iy], lsem.at[5]),
        pltpu.make_async_copy(delta_h, dl, lsem.at[6]),
        pltpu.make_async_copy(gcol_h, gcol, lsem.at[7]),
        pltpu.make_async_copy(live_h, glive, lsem.at[8]),
        pltpu.make_async_copy(prec_h, gprec, lsem.at[9]),
        pltpu.make_async_copy(w_h, wv, lsem.at[10]),
        pltpu.make_async_copy(obs_h, ob.at[iq], lsem.at[11]),
    ]
    for copy in local:
        copy.start()

    def remote(src, dst, send, recv, gx, gy):
        return pltpu.make_async_remote_copy(
            src_ref=src,
            dst_ref=dst,
            send_sem=send,
            recv_sem=recv,
            device_id={"gx": gx, "gy": gy},
            device_id_type=MESH,
        )

    def alpha_out(t):
        return remote(alpha_h, al.at[iy], asend.at[t], arecv.at[iy], ix, t)

    def alpha_in(t):
        return remote(alpha_h, al.at[t], asend.at[t], arecv.at[t], ix, t)

    def obs_out(q):
        return remote(obs_h, ob.at[iq], osend.at[q], orecv.at[iq], q * 4 + im, iy)

    def obs_in(q):
        return remote(obs_h, ob.at[q], osend.at[q], orecv.at[q], q * 4 + im, iy)

    def index_out(m):
        return remote(qi.at[im], qi.at[im], qsend.at[m], qrecv.at[im], iq * 4 + m, iy)

    def index_in(m):
        return remote(qi.at[m], qi.at[m], qsend.at[m], qrecv.at[m], iq * 4 + m, iy)

    def value_out(m):
        return remote(vo.at[m], vi.at[im], wsend.at[m], wrecv.at[im], iq * 4 + m, iy)

    def value_in(m):
        return remote(vo.at[m], vi.at[m], wsend.at[m], wrecv.at[m], iq * 4 + m, iy)

    def sums_out(t):
        return remote(sums.at[t], rsums.at[iy], ssend.at[t], srecv.at[iy], ix, t)

    def sums_in(t):
        return remote(sums.at[t], rsums.at[t], ssend.at[t], srecv.at[t], ix, t)

    def among(count, where, act):
        for t in range(count):

            @pl.when(where(t))
            def _():
                act(t)

    def not_y(t):
        return t != iy

    def not_m(m):
        return m != im

    pl.semaphore_wait(barrier, expected)
    among(16, not_y, lambda t: alpha_out(t).start())
    among(8, lambda q: q < iq, lambda q: obs_out(q).start())

    def halo_copy(ref, d, width, sends, receives):
        dx, dy = DIRS[d]
        if dx != 0 and dy != 0:
            width = width - 1
        gx, gy = ix + dx, iy + dy
        return remote(
            ref.at[:, inner_part(dx, X0, X1, width), inner_part(dy, Y0, Y1, width)],
            ref.at[:, outer_part(-dx, X0, X1, width), outer_part(-dy, Y0, Y1, width)],
            sends.at[d],
            receives.at[d],
            gx,
            gy,
        )

    def each(make, act, back):
        for d in range(8):
            dx, dy = DIRS[d]
            here = DIRS.index((-dx, -dy)) if back else d

            @pl.when(there(here))
            def _():
                act(make(d))

    def start(copy):
        copy.start()

    def wait_send(copy):
        copy.wait_send()

    def wait_recv(copy):
        copy.wait_recv()

    def coef_copy(d):
        return halo_copy(cf, d, 2, csend, crecv)

    def state_copy(d):
        return halo_copy(v0, d, 3, hsend, hrecv)

    local[0].wait()
    local[1].wait()
    each(coef_copy, start, False)
    local[2].wait()
    local[3].wait()
    among(4, not_m, lambda m: index_out(m).start())

    def zero(ref, x, y):
        ref[:, x[0] : x[1], y[0] : y[1]] = jnp.zeros((ref.shape[0], x[1] - x[0], y[1] - y[0], 128), f32)

    def missing(ref, width):
        for d, (dx, dy) in enumerate(DIRS):
            wide = width - 1 if dx != 0 and dy != 0 else width
            spans = []
            for sign, lo, hi in ((dx, X0, X1), (dy, Y0, Y1)):
                spans.append((hi, hi + wide) if sign > 0 else (lo - wide, lo) if sign < 0 else (lo, hi))

            @pl.when(jnp.logical_not(there(d)))
            def _():
                zero(ref, *spans)

    missing(cf, 2)
    missing(v0, 3)
    zero(cf, (0, 2), (0, YB))
    zero(cf, (22, XB), (0, YB))
    zero(cf, (2, 22), (0, 6))
    zero(cf, (2, 22), (26, YB))
    for x in (2, 21):
        zero(cf, (x, x + 1), (6, 8))
        zero(cf, (x, x + 1), (24, 26))
    for x in (3, 20):
        zero(cf, (x, x + 1), (6, 7))
        zero(cf, (x, x + 1), (25, 26))

    local[4].wait()
    lane = lax.broadcasted_iota(jnp.int32, (256, 128), 1)
    row = lax.broadcasted_iota(jnp.int32, (256, 128), 0)
    lanes = lane.astype(f32)
    up = lax.broadcasted_iota(jnp.int32, (256, 256), 0).astype(f32)
    of_row = jnp.where(row // 16 == lane, 1.0, 0.0).astype(bf16)
    tiles = jnp.concatenate(
        [
            jnp.concatenate([tm[...].astype(f32), jnp.zeros((16, 112), f32)], axis=1),
            jnp.zeros((112, 128), f32),
        ],
        axis=0,
    ).astype(bf16)
    picked = jnp.where(row % 16 == lane, dot(of_row, tiles), 0.0).astype(bf16)
    tile_at = dot(picked, jnp.ones((128, 128), bf16)) * 4.0

    def hot(values):
        return jnp.concatenate(
            [jnp.where(values == lanes, 1.0, 0.0), jnp.where(values == lanes + 128.0, 1.0, 0.0)], axis=1
        ).astype(bf16)

    for c in range(4):
        sel[c * 256 : (c + 1) * 256] = hot(tile_at + float(c))
    tile_row = tile_at.T[0:1]
    for c in range(4):
        selt[:, c * 256 : (c + 1) * 256] = jnp.where(up == tile_row + float(c), 1.0, 0.0).astype(bf16)
    for copy in local[5:11]:
        copy.wait()

    among(16, not_y, lambda t: alpha_in(t).wait_recv())
    high, low = split(al[...].reshape(256, 128))
    both = jnp.concatenate([high, low], axis=1)
    for c in range(4):
        product = dot(sel[c * 256 : (c + 1) * 256], both)
        profile = (product[:, :128] + product[:, 128:]).reshape(16, 16, 128)
        v0[c, X0:X1, Y0:Y1] = dl[c] + 0.125 * profile
    each(state_copy, start, False)

    def answer(q):
        obs_in(q).wait_recv()
        obs_out(q).start()

    among(8, lambda q: q > iq, answer)
    slot_column = gcol[0:1].astype(f32)
    oh[...] = jnp.where(up == slot_column, 1.0, 0.0).T.astype(bf16)
    for c in range(4):
        weight = wv[:, c, :]
        high, low = split(weight)
        wc[c] = weight
        w2[:, c * 128 : (c + 1) * 128] = high
        w2[:, 512 + c * 128 : 640 + c * 128] = low
    rx_rows = ((0, 3), (3, 6))
    for d, x in ((0, rx_rows[1]), (1, rx_rows[0])):

        @pl.when(jnp.logical_not(there(d)))
        def _():
            zero(rx, x, (0, 16))

    zero(ry, (0, 16), (3, 13))
    for d, y in ((2, (13, 16)), (3, (0, 3))):

        @pl.when(jnp.logical_not(there(d)))
        def _():
            zero(ry, (0, 16), y)

    zero(rc, (0, 4), (2, 14))
    for d in (4, 5, 6, 7):
        dx, dy = DIRS[d]

        @pl.when(jnp.logical_not(there(d)))
        def _():
            zero(rc, (2, 4) if dx > 0 else (0, 2), (14, 16) if dy > 0 else (0, 2))

    for ref in (a1, a2, a3):
        zero(ref, (0, X0), (0, YB))
        zero(ref, (X1, XB), (0, YB))
        zero(ref, (X0, X1), (0, Y0))
        zero(ref, (X0, X1), (Y1, YB))

    each(coef_copy, wait_recv, True)

    def derive(x, carry):
        e = cf[0, x]
        half_x = 0.5 * cf[1, x]
        half_y = 0.5 * cf[2, x]
        k5[0, x] = 1.0 - 4.0 * e
        k5[1, x] = e - half_x
        k5[2, x] = e + half_x
        k5[3, x] = e - half_y
        k5[4, x] = e + half_y
        return carry

    lax.fori_loop(0, XB, derive, 0)

    among(4, not_m, lambda m: index_in(m).wait_recv())
    local[11].wait()
    among(8, lambda q: q < iq, lambda q: obs_in(q).wait_recv())
    turned = [split(ob[:, step].reshape(64, 128).T) for step in range(STEPS)]
    table = jnp.concatenate([h for h, _ in turned] + [l for _, l in turned], axis=0)
    down64 = lax.broadcasted_iota(jnp.int32, (64, 256), 0)
    down128 = lax.broadcasted_iota(jnp.int32, (128, 256), 0)
    for m in range(4):
        beams = qi[m, 0:1]
        held = jnp.where((beams // 8) % 4 == im, (beams // 32) * 8 + beams % 8, -1)
        found = dot(table, jnp.where(down64 == held, 1.0, 0.0).astype(bf16))
        at_gate = down128 == qi[m, 1:2]
        for step in range(STEPS):
            both = found[step * 128 : (step + 1) * 128] + found[384 + step * 128 : 512 + step * 128]
            vo[m, step : step + 1] = jnp.sum(jnp.where(at_gate, both, 0.0), axis=0, keepdims=True)
    among(4, not_m, lambda m: value_out(m).start())

    each(state_copy, wait_recv, True)

    def forward(src, dst, margin):
        y0, rows = (Y0, 16) if margin == 0 else (4, 24)

        def body(x, carry):
            mid = pl.ds(y0, rows)
            dst[:, x, mid] = (
                k5[0, x, mid] * src[:, x, mid]
                + k5[1, x, mid] * src[:, x + 1, mid]
                + k5[2, x, mid] * src[:, x - 1, mid]
                + k5[3, x, mid] * src[:, x, pl.ds(y0 + 1, rows)]
                + k5[4, x, mid] * src[:, x, pl.ds(y0 - 1, rows)]
            )
            return carry

        lax.fori_loop(X0 - margin, X1 + margin, body, 0)

    def backward(src, dst, margin, extra):
        y0, rows = 4, 24

        def body(x, carry):
            mid = pl.ds(y0, rows)
            below = pl.ds(y0 - 1, rows)
            above = pl.ds(y0 + 1, rows)
            dst[:, x, mid] = (
                k5[0, x, mid] * src[:, x, mid]
                + k5[1, x - 1, mid] * src[:, x - 1, mid]
                + k5[2, x + 1, mid] * src[:, x + 1, mid]
                + k5[3, x, below] * src[:, x, below]
                + k5[4, x, above] * src[:, x, above]
            )
            return carry

        lax.fori_loop(X0 - margin, X1 + margin, body, 0)
        if extra is not None:
            for c in range(4):
                dst[c, X0:X1, Y0:Y1] += extra[c]

    ones = jnp.ones((8, 128), bf16)

    def along(value):
        return lax.dot_general(ones, value, (((1,), (1,)), ((), ())), preferred_element_type=f32)[0:1]

    def looked(state):
        parts = [split(state[c, X0:X1, Y0:Y1].reshape(256, 128)) for c in range(4)]
        product = dot(oh[...], jnp.concatenate([h for h, _ in parts] + [l for _, l in parts], axis=1))
        total = None
        for c in range(4):
            term = (product[:, c * 128 : (c + 1) * 128] + product[:, 512 + c * 128 : 640 + c * 128]) * wc[c]
            total = term if total is None else total + term
        high, low = split(total)
        return along(high) + along(low)

    forward(v0, v1, 2)
    seen = [looked(v1)]
    forward(v1, v2, 1)
    seen.append(looked(v2))
    forward(v2, v3, 0)
    seen.append(looked(v3))

    among(4, not_m, lambda m: value_in(m).wait_recv())
    vi[im] = vo[im]
    scale = glive[...].astype(f32) * gprec[...]
    mask = up == slot_column

    def forcing(step):
        observed = vi[0, step : step + 1] + vi[1, step : step + 1] + vi[2, step : step + 1] + vi[3, step : step + 1]
        misfit = scale * (seen[step] - observed)
        coarse = misfit.astype(bf16).astype(f32)
        fine = misfit - coarse
        wide = dot(jnp.where(mask, coarse, 0.0).astype(bf16), w2[...])
        rest = dot(jnp.where(mask, fine, 0.0).astype(bf16), w2[:, :512])
        return [
            (
                wide[:, c * 128 : (c + 1) * 128]
                + wide[:, 512 + c * 128 : 640 + c * 128]
                + rest[:, c * 128 : (c + 1) * 128]
            ).reshape(16, 16, 128)
            for c in range(4)
        ]

    last = forcing(2)
    for c in range(4):
        a3[c, X0:X1, Y0:Y1] = last[c]
    backward(a3, a2, 1, forcing(1))
    backward(a2, a1, 2, forcing(0))
    backward(a1, v1, 3, None)

    def push_copy(d):
        dx, dy = DIRS[d]
        width = 2 if dx != 0 and dy != 0 else 3
        src = v1.at[:, outer_part(dx, X0, X1, width), outer_part(dy, Y0, Y1, width)]
        at_y = inner_part(-dy, 0, 16, width)
        if dy == 0:
            dst = rx.at[:, inner_part(-dx, 0, 6, width)]
        elif dx == 0:
            dst = ry.at[:, :, at_y]
        else:
            dst = rc.at[:, inner_part(-dx, 0, 4, width), at_y]
        return remote(src, dst, psend.at[d], precv.at[d], ix + dx, iy + dy)

    each(push_copy, start, False)
    each(push_copy, wait_recv, True)
    total = None
    for c in range(4):
        v3[c, X0:X1, Y0:Y1] = v1[c, X0:X1, Y0:Y1] + ry[c]
        v3[c, X0 : X0 + 3, Y0:Y1] += rx[c, 0:3]
        v3[c, X1 - 3 : X1, Y0:Y1] += rx[c, 3:6]
        v3[c, X0 : X0 + 2, Y0:Y1] += rc[c, 0:2]
        v3[c, X1 - 2 : X1, Y0:Y1] += rc[c, 2:4]
        high, low = split(v3[c, X0:X1, Y0:Y1].reshape(256, 128))
        product = dot(selt[:, c * 256 : (c + 1) * 256], jnp.concatenate([high, low], axis=1))
        term = product[:, :128] + product[:, 128:]
        total = term if total is None else total + term
    sums[...] = total.reshape(16, 16, 128)
    among(16, not_y, lambda t: sums_out(t).start())
    rsums[iy] = sums[iy]
    for c in range(4):
        out_d[c] = dl[c] + v3[c, X0:X1, Y0:Y1]
    among(16, not_y, lambda t: alpha_out(t).wait_send())
    among(8, lambda q: q != iq, lambda q: obs_out(q).wait_send())
    among(4, not_m, lambda m: index_out(m).wait_send())
    among(4, not_m, lambda m: value_out(m).wait_send())
    each(coef_copy, wait_send, False)
    each(state_copy, wait_send, False)
    each(push_copy, wait_send, False)
    among(16, not_y, lambda t: sums_in(t).wait_recv())
    result = al[iy] + 0.125 * jnp.sum(rsums[...], axis=0)
    for t in range(4):
        out_a[t] = result[4 * t : 4 * t + 4]
    among(16, not_y, lambda t: sums_out(t).wait_send())


def on_device(
    delta, alpha, eddy, courant, tile_map, obs_rows,
    gate_beam, gate_index, gate_column, gate_live, obs_weight, obs_precision,
):
    dma = pltpu.SemaphoreType.DMA
    vm = pltpu.VMEM
    frame = vm((4, XB, YB, 128), f32)
    slots = vm((1, 256), jnp.int32)
    anywhere = pl.BlockSpec(memory_space=pl.ANY)
    inside = pl.BlockSpec(memory_space=pltpu.VMEM)
    row = (1, 256)
    adjoint, grad_alpha = pl.pallas_call(
        kernel,
        out_shape=(
            jax.ShapeDtypeStruct((4, 16, 16, 128), f32),
            jax.ShapeDtypeStruct((4, 4, 128), f32),
        ),
        in_specs=[anywhere] * 12,
        out_specs=(inside, inside),
        scratch_shapes=[
            vm((4, 16, 16, 128), f32),
            vm((3, XB, YB, 128), f32),
            vm((5, XB, YB, 128), f32),
            frame, frame, frame, frame,
            frame, frame, frame,
            vm((256, 4, 128), f32),
            vm((4, 256, 128), f32),
            vm((256, 1024), bf16),
            vm((16, 16), jnp.int32),
            vm((8, 3, 8, 128), f32),
            vm((4, 2, 256), jnp.int32),
            vm((4, 3, 256), f32),
            vm((4, 3, 256), f32),
            slots, slots,
            vm((1, 256), f32),
            vm((16, 16, 128), f32),
            vm((16, 16, 128), f32),
            vm((16, 16, 128), f32),
            vm((4, 6, 16, 128), f32),
            vm((4, 16, 16, 128), f32),
            vm((4, 4, 16, 128), f32),
            vm((256, 256), bf16),
            vm((1024, 256), bf16),
            vm((256, 1024), bf16),
            dma((12,)),
            dma((16,)), dma((16,)),
            dma((8,)), dma((8,)),
            dma((4,)), dma((4,)),
            dma((4,)), dma((4,)),
            dma((8,)), dma((8,)),
            dma((8,)), dma((8,)),
            dma((8,)), dma((8,)),
            dma((16,)), dma((16,)),
        ],
        compiler_params=pltpu.CompilerParams(
            collective_id=0, has_side_effects=True, vmem_limit_bytes=60 * 1024 * 1024
        ),
    )(
        delta,
        alpha.reshape(16, 128),
        eddy,
        courant,
        tile_map,
        obs_rows.transpose(1, 0, 2),
        gate_beam.reshape(row),
        gate_index.reshape(row),
        gate_column.reshape(row),
        gate_live.reshape(row),
        obs_weight.reshape(256, 4, 128),
        obs_precision.reshape(row),
    )
    return adjoint, grad_alpha.reshape(1, 4, 4, 128)


def solution(mesh):
    return jax.shard_map(
        on_device,
        mesh=mesh,
        in_specs=(
            P(None, "gx", "gy", None),
            P("gx", "gy", None, None),
            P("gx", "gy", None),
            P(None, "gx", "gy", None),
            P("gx", "gy"),
            P(("gx", "gy"), None, None),
            P("gx", "gy", None),
            P("gx", "gy", None),
            P("gx", "gy", None),
            P("gx", "gy", None),
            P("gx", "gy", None, None, None),
            P("gx", "gy", None),
        ),
        out_specs=(P(None, "gx", "gy", None), P("gx", "gy", None, None)),
        check_vma=False,
    )
```

time: 59.1 us -> 47.5 us (0.80)
  the two profiles are of different devices: /device:TPU:9 before, /device:TPU:481 now
where the time goes in v2:
time: 47.5 us; the launch traced here: 47.2 us
  Pallas kernels  44 us (93%)
  local copies, waits for them, and re-layouts  2.48 us (5%)
  between operations  0.65 us (1%)
    pallas_call x1, Pallas kernels, on_device(): pl.pallas_call(kernel, out_shape=(jax.ShapeDtypeStruct((4, 16, 16, 128),...  44 us
    unnamed x4, local copies, waits for them, and re-layouts  2.48 us

profile of v2, /device:TPU:481, one launch (start us, length us, event | category | flops | bytes accessed | tf_op | source)
XLA Modules:
  0.0 47.2 jit_solution(9298562145740358398)
XLA Ops:
  0.6 44.0 %shard_map.131 = (f32[4,16,16,128]{3,2,1,0:T(8,128)}, f32[4,4,128]{2,1,0:T(4,128)}) custom-call(f32[4,16,16,128]{3,2,1,0:T(8,128)} %delta_h.1, f32[16,128]{1,0:T(8,128)} %bitcast.11, f32[16,16,128]{2,1,0:T(8,128)} %eddy_h.1, f32[2,16,16,128]{3,2,1,0:T(8,128)} %courant_h.1, s32[16,16]{1,0:T(8,128)} %tmap_h.1, f32[3,8,128]{2,1,0:T(8,128)} %bitcast.10, ...), custom_call_target="tpu_custom_call" | custom-call | tf_op jit(solution)/shard_map/pallas_call | solution.py:513
  44.7 0.0 copy-start
  44.7 1.9 %copy.16 = f32[4,16,16,128]{3,2,1,0:T(8,128)} copy(f32[4,16,16,128]{3,2,1,0:T(8,128)} %get-tuple-element.8) | data formatting | bytes 1048576
  46.6 0.0 copy-done
  46.6 0.6 %copy.17 = f32[1,4,4,128]{3,2,1,0:T(4,128)} copy(f32[1,4,4,128]{3,2,1,0:T(4,128)S(1)} %bitcast.12) | data formatting | bytes 16384
Async XLA Ops:
  44.7 1.9 %copy-start = (f32[4,4,128]{2,1,0:T(4,128)S(1)}, f32[4,4,128]{2,1,0:T(4,128)}, u32[]{:S(2)}) copy-start(f32[4,4,128]{2,1,0:T(4,128)} %get-tuple-element.5) | copy-start | bytes 24580

commit v3 on v2

--- a/solution.py
+++ b/solution.py
@@ -16,6 +16,10 @@
 DIRS = [(1, 0), (-1, 0), (0, 1), (0, -1), (1, 1), (1, -1), (-1, 1), (-1, -1)]
 
 
+EDGES = (0, 1, 4, 5, 6, 7)
+SIDES = (2, 3)
+
+
 def inner_part(sign, lo, hi, width):
     if sign > 0:
         return pl.ds(hi - width, width)
@@ -42,10 +46,15 @@
     return jnp.dot(a, b, preferred_element_type=f32)
 
 
+AT_ONCE = ((), (0,), (0, 1), (0, 1, 2), (0, 1, 2, 3, 5, 6), (0, 1, 2, 3, 4, 6, 7), (0, 1, 4, 5, 7), (0, 1, 2, 5, 6))
+THROUGH = ((), (), (), (), ((5, 7),), (), ((5, 3), (4, 2)), ((6, 4), (5, 3)))
+ANSWER = tuple(tuple(range(q + 1, 8)) if q < 4 else () for q in range(8))
+
+
 def kernel(
     delta_h, alpha_h, eddy_h, courant_h, tmap_h, obs_h, beam_h, gidx_h, gcol_h, live_h, w_h, prec_h,
     out_d, out_a,
-    dl, cf, k5, v0, v1, v2, v3, a1, a2, a3, wv, wc, w2, tm, ob, qi, vo, vi, gcol, glive, gprec,
+    od, oa, dl, cf, k5, v0, v1, v2, v3, a1, a2, a3, wv, wc, w2, tm, ob, qi, vo, vi, gcol, glive, gprec,
     al, sums, rsums, rx, ry, rc,
     oh, sel, selt,
     lsem, asend, arecv, osend, orecv, qsend, qrecv, wsend, wrecv,
@@ -87,7 +96,10 @@
         def _():
             greet(ix, t)
 
-    expected = (ny - 1) + 3 + iq
+    greeted = 0
+    for q in range(8):
+        greeted = greeted + jnp.where(iq == q, len(AT_ONCE[q]), 0)
+    expected = (ny - 1) + 3 + greeted
     for d in (0, 1, 4, 5, 6, 7):
         ok = there(d)
 
@@ -102,25 +114,30 @@
         def _():
             greet(iq * 4 + m, iy)
 
-    for q in range(1, 8):
-
-        @pl.when(q > iq)
-        def _():
-            greet(q * 4 + im, iy)
+    def far(table, act):
+        for q in range(8):
+            if table[q]:
+
+                @pl.when(iq == q)
+                def _():
+                    for item in table[q]:
+                        act(item)
+
+    far([[r for r in range(8) if q in AT_ONCE[r]] for q in range(8)], lambda r: greet(r * 4 + im, iy))
 
     local = [
-        pltpu.make_async_copy(eddy_h, cf.at[0, X0:X1, Y0:Y1], lsem.at[0]),
-        pltpu.make_async_copy(courant_h, cf.at[pl.ds(1, 2), X0:X1, Y0:Y1], lsem.at[1]),
-        pltpu.make_async_copy(beam_h, qi.at[im, pl.ds(0, 1)], lsem.at[2]),
-        pltpu.make_async_copy(gidx_h, qi.at[im, pl.ds(1, 1)], lsem.at[3]),
-        pltpu.make_async_copy(tmap_h, tm, lsem.at[4]),
-        pltpu.make_async_copy(alpha_h, al.at[iy], lsem.at[5]),
-        pltpu.make_async_copy(delta_h, dl, lsem.at[6]),
+        pltpu.make_async_copy(alpha_h, al.at[iy], lsem.at[0]),
+        pltpu.make_async_copy(obs_h, ob.at[iq], lsem.at[1]),
+        pltpu.make_async_copy(eddy_h, cf.at[0, X0:X1, Y0:Y1], lsem.at[2]),
+        pltpu.make_async_copy(courant_h, cf.at[pl.ds(1, 2), X0:X1, Y0:Y1], lsem.at[3]),
+        pltpu.make_async_copy(beam_h, qi.at[im, pl.ds(0, 1)], lsem.at[4]),
+        pltpu.make_async_copy(gidx_h, qi.at[im, pl.ds(1, 1)], lsem.at[5]),
+        pltpu.make_async_copy(tmap_h, tm, lsem.at[6]),
         pltpu.make_async_copy(gcol_h, gcol, lsem.at[7]),
         pltpu.make_async_copy(live_h, glive, lsem.at[8]),
         pltpu.make_async_copy(prec_h, gprec, lsem.at[9]),
         pltpu.make_async_copy(w_h, wv, lsem.at[10]),
-        pltpu.make_async_copy(obs_h, ob.at[iq], lsem.at[11]),
+        pltpu.make_async_copy(delta_h, dl, lsem.at[11]),
     ]
     for copy in local:
         copy.start()
@@ -136,16 +153,16 @@
         )
 
     def alpha_out(t):
-        return remote(alpha_h, al.at[iy], asend.at[t], arecv.at[iy], ix, t)
+        return remote(al.at[iy], al.at[iy], asend.at[t], arecv.at[iy], ix, t)
 
     def alpha_in(t):
-        return remote(alpha_h, al.at[t], asend.at[t], arecv.at[t], ix, t)
+        return remote(al.at[t], al.at[t], asend.at[t], arecv.at[t], ix, t)
 
     def obs_out(q):
-        return remote(obs_h, ob.at[iq], osend.at[q], orecv.at[iq], q * 4 + im, iy)
+        return remote(ob.at[iq], ob.at[iq], osend.at[q], orecv.at[iq], q * 4 + im, iy)
 
     def obs_in(q):
-        return remote(obs_h, ob.at[q], osend.at[q], orecv.at[q], q * 4 + im, iy)
+        return remote(ob.at[q], ob.at[q], osend.at[q], orecv.at[q], q * 4 + im, iy)
 
     def index_out(m):
         return remote(qi.at[im], qi.at[im], qsend.at[m], qrecv.at[im], iq * 4 + m, iy)
@@ -172,15 +189,26 @@
             def _():
                 act(t)
 
-    def not_y(t):
-        return t != iy
+    ox = (iy // 2) % 4
+    others = []
+    for dy, dx in ((1, 2), (1, 1), (1, 3), (0, 2), (1, 0), (0, 1), (0, 3), (0, 0)):
+        for dc in (1, 0):
+            if (dy, dx, dc) != (0, 0, 0):
+                ty = (iy // 8 + dy) % 2
+                others.append(ty * 8 + ((ox + dx) % 4) * 2 + (iy + dc) % 2)
+
+    def strip(act):
+        for t in others:
+            act(t)
 
     def not_m(m):
         return m != im
 
+    local[0].wait()
+    local[1].wait()
     pl.semaphore_wait(barrier, expected)
-    among(16, not_y, lambda t: alpha_out(t).start())
-    among(8, lambda q: q < iq, lambda q: obs_out(q).start())
+    strip(lambda t: alpha_out(t).start())
+    far(AT_ONCE, lambda q: obs_out(q).start())
 
     def halo_copy(ref, d, width, sends, receives):
         dx, dy = DIRS[d]
@@ -196,8 +224,8 @@
             gy,
         )
 
-    def each(make, act, back):
-        for d in range(8):
+    def each(make, act, back, those=range(8)):
+        for d in those:
             dx, dy = DIRS[d]
             here = DIRS.index((-dx, -dy)) if back else d
 
@@ -220,11 +248,11 @@
     def state_copy(d):
         return halo_copy(v0, d, 3, hsend, hrecv)
 
-    local[0].wait()
-    local[1].wait()
-    each(coef_copy, start, False)
     local[2].wait()
     local[3].wait()
+    each(coef_copy, start, False)
+    local[4].wait()
+    local[5].wait()
     among(4, not_m, lambda m: index_out(m).start())
 
     def zero(ref, x, y):
@@ -254,7 +282,7 @@
         zero(cf, (x, x + 1), (6, 7))
         zero(cf, (x, x + 1), (25, 26))
 
-    local[4].wait()
+    local[6].wait()
     lane = lax.broadcasted_iota(jnp.int32, (256, 128), 1)
     row = lax.broadcasted_iota(jnp.int32, (256, 128), 0)
     lanes = lane.astype(f32)
@@ -280,31 +308,20 @@
     tile_row = tile_at.T[0:1]
     for c in range(4):
         selt[:, c * 256 : (c + 1) * 256] = jnp.where(up == tile_row + float(c), 1.0, 0.0).astype(bf16)
-    for copy in local[5:11]:
+    for copy in local[7:12]:
         copy.wait()
 
-    among(16, not_y, lambda t: alpha_in(t).wait_recv())
-    high, low = split(al[...].reshape(256, 128))
-    both = jnp.concatenate([high, low], axis=1)
-    for c in range(4):
-        product = dot(sel[c * 256 : (c + 1) * 256], both)
-        profile = (product[:, :128] + product[:, 128:]).reshape(16, 16, 128)
-        v0[c, X0:X1, Y0:Y1] = dl[c] + 0.125 * profile
-    each(state_copy, start, False)
-
-    def answer(q):
-        obs_in(q).wait_recv()
-        obs_out(q).start()
-
-    among(8, lambda q: q > iq, answer)
     slot_column = gcol[0:1].astype(f32)
-    oh[...] = jnp.where(up == slot_column, 1.0, 0.0).T.astype(bf16)
+    at_slot = jnp.where(up == slot_column, 1.0, 0.0).T.astype(bf16)
+    oh[:, :256] = at_slot
+    oh[:, 256:] = at_slot
     for c in range(4):
         weight = wv[:, c, :]
         high, low = split(weight)
         wc[c] = weight
-        w2[:, c * 128 : (c + 1) * 128] = high
-        w2[:, 512 + c * 128 : 640 + c * 128] = low
+        w2[0:256, c * 128 : (c + 1) * 128] = high
+        w2[256:512, c * 128 : (c + 1) * 128] = low
+        w2[512:768, c * 128 : (c + 1) * 128] = high
     rx_rows = ((0, 3), (3, 6))
     for d, x in ((0, rx_rows[1]), (1, rx_rows[0])):
 
@@ -332,6 +349,28 @@
         zero(ref, (X1, XB), (0, YB))
         zero(ref, (X0, X1), (0, Y0))
         zero(ref, (X0, X1), (Y1, YB))
+
+    def through(item):
+        obs_in(item[0]).wait_recv()
+        obs_out(item[1]).start()
+
+    far(THROUGH, through)
+
+    strip(lambda t: alpha_in(t).wait_recv())
+    high, low = split(al[...].reshape(256, 128))
+    both = jnp.concatenate([high, low], axis=1)
+
+    def state_rows(x0, x1):
+        for c in range(4):
+            product = dot(sel[c * 256 + x0 * 16 : c * 256 + x1 * 16], both)
+            profile = (product[:, :128] + product[:, 128:]).reshape(x1 - x0, 16, 128)
+            v0[c, X0 + x0 : X0 + x1, Y0:Y1] = dl[c, x0:x1] + 0.125 * profile
+
+    state_rows(0, 3)
+    state_rows(13, 16)
+    each(state_copy, start, False, EDGES)
+    state_rows(3, 13)
+    each(state_copy, start, False, SIDES)
 
     each(coef_copy, wait_recv, True)
 
@@ -348,20 +387,26 @@
 
     lax.fori_loop(0, XB, derive, 0)
 
+    def answer(q):
+        obs_in(q).wait_recv()
+        obs_out(q).start()
+
+    far(ANSWER, answer)
     among(4, not_m, lambda m: index_in(m).wait_recv())
-    local[11].wait()
-    among(8, lambda q: q < iq, lambda q: obs_in(q).wait_recv())
+    waited = [[t for t, _ in THROUGH[q]] + list(ANSWER[q]) + [q] for q in range(8)]
+    far([[r for r in range(8) if r not in waited[q]] for q in range(8)], lambda q: obs_in(q).wait_recv())
     turned = [split(ob[:, step].reshape(64, 128).T) for step in range(STEPS)]
-    table = jnp.concatenate([h for h, _ in turned] + [l for _, l in turned], axis=0)
+    table = jnp.concatenate([jnp.concatenate(pair, axis=1) for pair in turned], axis=0)
     down64 = lax.broadcasted_iota(jnp.int32, (64, 256), 0)
     down128 = lax.broadcasted_iota(jnp.int32, (128, 256), 0)
     for m in range(4):
         beams = qi[m, 0:1]
         held = jnp.where((beams // 8) % 4 == im, (beams // 32) * 8 + beams % 8, -1)
-        found = dot(table, jnp.where(down64 == held, 1.0, 0.0).astype(bf16))
+        at_beam = jnp.where(down64 == held, 1.0, 0.0).astype(bf16)
+        found = dot(table, jnp.concatenate([at_beam, at_beam], axis=0))
         at_gate = down128 == qi[m, 1:2]
         for step in range(STEPS):
-            both = found[step * 128 : (step + 1) * 128] + found[384 + step * 128 : 512 + step * 128]
+            both = found[step * 128 : (step + 1) * 128]
             vo[m, step : step + 1] = jnp.sum(jnp.where(at_gate, both, 0.0), axis=0, keepdims=True)
     among(4, not_m, lambda m: value_out(m).start())
 
@@ -383,7 +428,7 @@
 
         lax.fori_loop(X0 - margin, X1 + margin, body, 0)
 
-    def backward(src, dst, margin, extra):
+    def backward(src, dst, first, last, extra):
         y0, rows = 4, 24
 
         def body(x, carry):
@@ -399,7 +444,7 @@
             )
             return carry
 
-        lax.fori_loop(X0 - margin, X1 + margin, body, 0)
+        lax.fori_loop(first, last, body, 0)
         if extra is not None:
             for c in range(4):
                 dst[c, X0:X1, Y0:Y1] += extra[c]
@@ -411,10 +456,11 @@
 
     def looked(state):
         parts = [split(state[c, X0:X1, Y0:Y1].reshape(256, 128)) for c in range(4)]
-        product = dot(oh[...], jnp.concatenate([h for h, _ in parts] + [l for _, l in parts], axis=1))
+        halves = [jnp.concatenate([part[k] for part in parts], axis=1) for k in range(2)]
+        product = dot(oh[...], jnp.concatenate(halves, axis=0))
         total = None
         for c in range(4):
-            term = (product[:, c * 128 : (c + 1) * 128] + product[:, 512 + c * 128 : 640 + c * 128]) * wc[c]
+            term = product[:, c * 128 : (c + 1) * 128] * wc[c]
             total = term if total is None else total + term
         high, low = split(total)
         return along(high) + along(low)
@@ -436,23 +482,18 @@
         misfit = scale * (seen[step] - observed)
         coarse = misfit.astype(bf16).astype(f32)
         fine = misfit - coarse
-        wide = dot(jnp.where(mask, coarse, 0.0).astype(bf16), w2[...])
-        rest = dot(jnp.where(mask, fine, 0.0).astype(bf16), w2[:, :512])
-        return [
-            (
-                wide[:, c * 128 : (c + 1) * 128]
-                + wide[:, 512 + c * 128 : 640 + c * 128]
-                + rest[:, c * 128 : (c + 1) * 128]
-            ).reshape(16, 16, 128)
-            for c in range(4)
-        ]
+        high = jnp.where(mask, coarse, 0.0).astype(bf16)
+        low = jnp.where(mask, fine, 0.0).astype(bf16)
+        product = dot(jnp.concatenate([high, high, low], axis=1), w2[...])
+        return [product[:, c * 128 : (c + 1) * 128].reshape(16, 16, 128) for c in range(4)]
 
     last = forcing(2)
     for c in range(4):
         a3[c, X0:X1, Y0:Y1] = last[c]
-    backward(a3, a2, 1, forcing(1))
-    backward(a2, a1, 2, forcing(0))
-    backward(a1, v1, 3, None)
+    backward(a3, a2, X0 - 1, X1 + 1, forcing(1))
+    backward(a2, a1, X0 - 2, X1 + 2, forcing(0))
+    backward(a1, v1, X0 - 3, X0, None)
+    backward(a1, v1, X1, X1 + 3, None)
 
     def push_copy(d):
         dx, dy = DIRS[d]
@@ -467,7 +508,9 @@
             dst = rc.at[:, inner_part(-dx, 0, 4, width), at_y]
         return remote(src, dst, psend.at[d], precv.at[d], ix + dx, iy + dy)
 
-    each(push_copy, start, False)
+    each(push_copy, start, False, EDGES)
+    backward(a1, v1, X0, X1, None)
+    each(push_copy, start, False, SIDES)
     each(push_copy, wait_recv, True)
     total = None
     for c in range(4):
@@ -481,22 +524,36 @@
         term = product[:, :128] + product[:, 128:]
         total = term if total is None else total + term
     sums[...] = total.reshape(16, 16, 128)
-    among(16, not_y, lambda t: sums_out(t).start())
+    strip(lambda t: sums_out(t).start())
     rsums[iy] = sums[iy]
     for c in range(4):
-        out_d[c] = dl[c] + v3[c, X0:X1, Y0:Y1]
-    among(16, not_y, lambda t: alpha_out(t).wait_send())
+        od[c] = dl[c] + v3[c, X0:X1, Y0:Y1]
+    leave_d = pltpu.make_async_copy(od, out_d, lsem.at[0])
+    leave_d.start()
+    strip(lambda t: alpha_out(t).wait_send())
     among(8, lambda q: q != iq, lambda q: obs_out(q).wait_send())
     among(4, not_m, lambda m: index_out(m).wait_send())
     among(4, not_m, lambda m: value_out(m).wait_send())
     each(coef_copy, wait_send, False)
     each(state_copy, wait_send, False)
     each(push_copy, wait_send, False)
-    among(16, not_y, lambda t: sums_in(t).wait_recv())
+    strip(lambda t: sums_in(t).wait_recv())
     result = al[iy] + 0.125 * jnp.sum(rsums[...], axis=0)
     for t in range(4):
-        out_a[t] = result[4 * t : 4 * t + 4]
-    among(16, not_y, lambda t: sums_out(t).wait_send())
+        oa[t] = result[4 * t : 4 * t + 4]
+    leave_a = pltpu.make_async_copy(oa, out_a, lsem.at[1])
+    leave_a.start()
+    strip(lambda t: sums_out(t).wait_send())
+    leave_d.wait()
+    leave_a.wait()
+
+
+def hand_on(d_ref, a_ref, out_d, out_a, sems):
+    copies = [pltpu.make_async_copy(d_ref, out_d, sems.at[0]), pltpu.make_async_copy(a_ref, out_a, sems.at[1])]
+    for copy in copies:
+        copy.start()
+    for copy in copies:
+        copy.wait()
 
 
 def on_device(
@@ -508,17 +565,18 @@
     frame = vm((4, XB, YB, 128), f32)
     slots = vm((1, 256), jnp.int32)
     anywhere = pl.BlockSpec(memory_space=pl.ANY)
-    inside = pl.BlockSpec(memory_space=pltpu.VMEM)
     row = (1, 256)
-    adjoint, grad_alpha = pl.pallas_call(
+    grad_delta, grad_alpha = pl.pallas_call(
         kernel,
         out_shape=(
             jax.ShapeDtypeStruct((4, 16, 16, 128), f32),
             jax.ShapeDtypeStruct((4, 4, 128), f32),
         ),
         in_specs=[anywhere] * 12,
-        out_specs=(inside, inside),
+        out_specs=(anywhere, anywhere),
         scratch_shapes=[
+            vm((4, 16, 16, 128), f32),
+            vm((4, 4, 128), f32),
             vm((4, 16, 16, 128), f32),
             vm((3, XB, YB, 128), f32),
             vm((5, XB, YB, 128), f32),
@@ -526,7 +584,7 @@
             frame, frame, frame,
             vm((256, 4, 128), f32),
             vm((4, 256, 128), f32),
-            vm((256, 1024), bf16),
+            vm((768, 512), bf16),
             vm((16, 16), jnp.int32),
             vm((8, 3, 8, 128), f32),
             vm((4, 2, 256), jnp.int32),
@@ -540,7 +598,7 @@
             vm((4, 6, 16, 128), f32),
             vm((4, 16, 16, 128), f32),
             vm((4, 4, 16, 128), f32),
-            vm((256, 256), bf16),
+            vm((256, 512), bf16),
             vm((1024, 256), bf16),
             vm((256, 1024), bf16),
             dma((12,)),
@@ -570,7 +628,18 @@
         obs_weight.reshape(256, 4, 128),
         obs_precision.reshape(row),
     )
-    return adjoint, grad_alpha.reshape(1, 4, 4, 128)
+    grad_delta, grad_alpha = pl.pallas_call(
+        hand_on,
+        out_shape=(
+            jax.ShapeDtypeStruct((4, 16, 16, 128), f32),
+            jax.ShapeDtypeStruct((4, 4, 128), f32),
+        ),
+        in_specs=[anywhere] * 2,
+        out_specs=(anywhere, anywhere),
+        scratch_shapes=[dma((2,))],
+        compiler_params=pltpu.CompilerParams(vmem_limit_bytes=60 * 1024 * 1024),
+    )(grad_delta, grad_alpha)
+    return grad_delta, grad_alpha.reshape(1, 4, 4, 128)
 
 
 def solution(mesh):

time: 47.5 us -> 64.2 us (1.35)
  Pallas kernels: 44 us -> 63.3 us
  local copies, waits for them, and re-layouts: 2.48 us -> 0 us
    pallas_call x0 -> x1, Pallas kernels: none -> 17.3 us  [on_device(): pl.pallas_call(hand_on, out_shape=(jax.ShapeDtypeStruct((4, 16, 16, 128),...]
    unnamed x4 -> x0, local copies, waits for them, and re-layouts: 2.48 us -> none
    pallas_call x1, Pallas kernels: 44 us -> 46 us  [on_device(): pl.pallas_call(kernel, out_shape=(jax.ShapeDtypeStruct((4, 16, 16, 128),...]
where the time goes in v3:
time: 64.2 us; the launch traced here: 63.9 us
  Pallas kernels  63.3 us (99%)
    pallas_call x1, Pallas kernels, on_device(): pl.pallas_call(kernel, out_shape=(jax.ShapeDtypeStruct((4, 16, 16, 128),...  46 us
    pallas_call x1, Pallas kernels, on_device(): pl.pallas_call(hand_on, out_shape=(jax.ShapeDtypeStruct((4, 16, 16, 128),...  17.3 us

profile of v3, /device:TPU:481, one launch (start us, length us, event | category | flops | bytes accessed | tf_op | source)
XLA Modules:
  0.0 63.9 jit_solution(8261892943200325907)
XLA Ops:
  0.6 46.0 %shard_map.131 = (f32[4,16,16,128]{3,2,1,0:T(8,128)}, f32[4,4,128]{2,1,0:T(4,128)}) custom-call(f32[4,16,16,128]{3,2,1,0:T(8,128)} %delta_h.1, f32[16,128]{1,0:T(8,128)} %bitcast.11, f32[16,16,128]{2,1,0:T(8,128)} %eddy_h.1, f32[2,16,16,128]{3,2,1,0:T(8,128)} %courant_h.1, s32[16,16]{1,0:T(8,128)} %tmap_h.1, f32[3,8,128]{2,1,0:T(8,128)} %bitcast.10, ...), custom_call_target="tpu_custom_call" | custom-call | tf_op jit(solution)/shard_map/pallas_call | solution.py:569
  46.6 17.3 %shard_map.132 = (f32[4,16,16,128]{3,2,1,0:T(8,128)}, f32[4,4,128]{2,1,0:T(4,128)}) custom-call(f32[4,16,16,128]{3,2,1,0:T(8,128)} %get-tuple-element.6.d_ref, f32[4,4,128]{2,1,0:T(4,128)} %get-tuple-element.7.a_ref), custom_call_target="tpu_custom_call" | custom-call | tf_op jit(solution)/shard_map/pallas_call | solution.py:631

commit v4 on v3

--- a/solution.py
+++ b/solution.py
@@ -48,13 +48,19 @@
 
 AT_ONCE = ((), (0,), (0, 1), (0, 1, 2), (0, 1, 2, 3, 5, 6), (0, 1, 2, 3, 4, 6, 7), (0, 1, 4, 5, 7), (0, 1, 2, 5, 6))
 THROUGH = ((), (), (), (), ((5, 7),), (), ((5, 3), (4, 2)), ((6, 4), (5, 3)))
-ANSWER = tuple(tuple(range(q + 1, 8)) if q < 4 else () for q in range(8))
+ANSWER = (
+    ((1, (1,)), (2, (2,)), (7, (7, 6, 5)), (6, (4,)), (3, (3,))),
+    ((2, (2,)), (3, (3,)), (7, (7, 6, 5)), (6, (4,))),
+    ((3, (3,)), (4, (4, 5, 6)), (5, (7,))),
+    ((4, (4, 6)), (5, (5, 7))),
+    (), (), (), (),
+)
 
 
 def kernel(
     delta_h, alpha_h, eddy_h, courant_h, tmap_h, obs_h, beam_h, gidx_h, gcol_h, live_h, w_h, prec_h,
     out_d, out_a,
-    od, oa, dl, cf, k5, v0, v1, v2, v3, a1, a2, a3, wv, wc, w2, tm, ob, qi, vo, vi, gcol, glive, gprec,
+    dl, cf, k5, v0, v1, v2, v3, a1, a2, a3, wv, wc, w2, tm, ob, qi, vo, vi, gcol, glive, gprec,
     al, sums, rsums, rx, ry, rc,
     oh, sel, selt,
     lsem, asend, arecv, osend, orecv, qsend, qrecv, wsend, wrecv,
@@ -372,6 +378,13 @@
     state_rows(3, 13)
     each(state_copy, start, False, SIDES)
 
+    def answer(item):
+        obs_in(item[0]).wait_recv()
+        for q in item[1]:
+            obs_out(q).start()
+
+    far([ANSWER[q] if q >= 2 else () for q in range(8)], answer)
+
     each(coef_copy, wait_recv, True)
 
     def derive(x, carry):
@@ -387,13 +400,9 @@
 
     lax.fori_loop(0, XB, derive, 0)
 
-    def answer(q):
-        obs_in(q).wait_recv()
-        obs_out(q).start()
-
-    far(ANSWER, answer)
+    far([ANSWER[q] if q < 2 else () for q in range(8)], answer)
     among(4, not_m, lambda m: index_in(m).wait_recv())
-    waited = [[t for t, _ in THROUGH[q]] + list(ANSWER[q]) + [q] for q in range(8)]
+    waited = [[t for t, _ in THROUGH[q] + ANSWER[q]] + [q] for q in range(8)]
     far([[r for r in range(8) if r not in waited[q]] for q in range(8)], lambda q: obs_in(q).wait_recv())
     turned = [split(ob[:, step].reshape(64, 128).T) for step in range(STEPS)]
     table = jnp.concatenate([jnp.concatenate(pair, axis=1) for pair in turned], axis=0)
@@ -527,9 +536,7 @@
     strip(lambda t: sums_out(t).start())
     rsums[iy] = sums[iy]
     for c in range(4):
-        od[c] = dl[c] + v3[c, X0:X1, Y0:Y1]
-    leave_d = pltpu.make_async_copy(od, out_d, lsem.at[0])
-    leave_d.start()
+        out_d[c] = dl[c] + v3[c, X0:X1, Y0:Y1]
     strip(lambda t: alpha_out(t).wait_send())
     among(8, lambda q: q != iq, lambda q: obs_out(q).wait_send())
     among(4, not_m, lambda m: index_out(m).wait_send())
@@ -540,20 +547,8 @@
     strip(lambda t: sums_in(t).wait_recv())
     result = al[iy] + 0.125 * jnp.sum(rsums[...], axis=0)
     for t in range(4):
-        oa[t] = result[4 * t : 4 * t + 4]
-    leave_a = pltpu.make_async_copy(oa, out_a, lsem.at[1])
-    leave_a.start()
+        out_a[t] = result[4 * t : 4 * t + 4]
     strip(lambda t: sums_out(t).wait_send())
-    leave_d.wait()
-    leave_a.wait()
-
-
-def hand_on(d_ref, a_ref, out_d, out_a, sems):
-    copies = [pltpu.make_async_copy(d_ref, out_d, sems.at[0]), pltpu.make_async_copy(a_ref, out_a, sems.at[1])]
-    for copy in copies:
-        copy.start()
-    for copy in copies:
-        copy.wait()
 
 
 def on_device(
@@ -565,18 +560,14 @@
     frame = vm((4, XB, YB, 128), f32)
     slots = vm((1, 256), jnp.int32)
     anywhere = pl.BlockSpec(memory_space=pl.ANY)
+    inside = pl.BlockSpec(memory_space=pltpu.VMEM)
     row = (1, 256)
     grad_delta, grad_alpha = pl.pallas_call(
         kernel,
-        out_shape=(
-            jax.ShapeDtypeStruct((4, 16, 16, 128), f32),
-            jax.ShapeDtypeStruct((4, 4, 128), f32),
-        ),
+        out_shape=(vm((4, 16, 16, 128), f32), vm((4, 4, 128), f32)),
         in_specs=[anywhere] * 12,
-        out_specs=(anywhere, anywhere),
+        out_specs=(inside, inside),
         scratch_shapes=[
-            vm((4, 16, 16, 128), f32),
-            vm((4, 4, 128), f32),
             vm((4, 16, 16, 128), f32),
             vm((3, XB, YB, 128), f32),
             vm((5, XB, YB, 128), f32),
@@ -628,17 +619,6 @@
         obs_weight.reshape(256, 4, 128),
         obs_precision.reshape(row),
     )
-    grad_delta, grad_alpha = pl.pallas_call(
-        hand_on,
-        out_shape=(
-            jax.ShapeDtypeStruct((4, 16, 16, 128), f32),
-            jax.ShapeDtypeStruct((4, 4, 128), f32),
-        ),
-        in_specs=[anywhere] * 2,
-        out_specs=(anywhere, anywhere),
-        scratch_shapes=[dma((2,))],
-        compiler_params=pltpu.CompilerParams(vmem_limit_bytes=60 * 1024 * 1024),
-    )(grad_delta, grad_alpha)
     return grad_delta, grad_alpha.reshape(1, 4, 4, 128)
 
 

time: 64.2 us -> 43.5 us (0.68)
  the two profiles are of different devices: /device:TPU:481 before, /device:TPU:121 now
where the time goes in v4:
time: 43.5 us; the launch traced here: 43.4 us
  Pallas kernels  41.3 us (95%)
  local copies, waits for them, and re-layouts  1.39 us (3%)
  between operations  0.64 us (1%)
    pallas_call x1, Pallas kernels, on_device(): pl.pallas_call(kernel, out_shape=(vm((4, 16, 16, 128), f32), vm((4, 4, 12...  41.3 us
    unnamed x2, local copies, waits for them, and re-layouts  1.39 us

profile of v4, /device:TPU:121, one launch (start us, length us, event | category | flops | bytes accessed | tf_op | source)
XLA Modules:
  0.0 43.4 jit_solution(10068811792789462641)
XLA Ops:
  0.6 41.3 %shard_map.131 = (f32[4,16,16,128]{3,2,1,0:T(8,128)S(1)}, f32[4,4,128]{2,1,0:T(4,128)S(1)}) custom-call(f32[4,16,16,128]{3,2,1,0:T(8,128)} %delta_h.1, f32[16,128]{1,0:T(8,128)} %bitcast.12, f32[16,16,128]{2,1,0:T(8,128)} %eddy_h.1, f32[2,16,16,128]{3,2,1,0:T(8,128)} %courant_h.1, s32[16,16]{1,0:T(8,128)} %tmap_h.1, f32[3,8,128]{2,1,0:T(8,128)} %bitcast.11, ...), custom_call_target="tpu_custom_call" | custom-call | tf_op jit(solution)/shard_map/pallas_call | solution.py:565
  42.0 0.8 %copy.16 = f32[4,16,16,128]{3,2,1,0:T(8,128)} copy(f32[4,16,16,128]{3,2,1,0:T(8,128)S(1)} %get-tuple-element.6) | data formatting | bytes 1048576
  42.8 0.6 %copy.17 = f32[1,4,4,128]{3,2,1,0:T(4,128)} copy(f32[1,4,4,128]{3,2,1,0:T(4,128)S(1)} %bitcast.9) | data formatting | bytes 16384

commit v5 on v4

--- a/solution.py
+++ b/solution.py
@@ -46,8 +46,8 @@
     return jnp.dot(a, b, preferred_element_type=f32)
 
 
-AT_ONCE = ((), (0,), (0, 1), (0, 1, 2), (0, 1, 2, 3, 5, 6), (0, 1, 2, 3, 4, 6, 7), (0, 1, 4, 5, 7), (0, 1, 2, 5, 6))
-THROUGH = ((), (), (), (), ((5, 7),), (), ((5, 3), (4, 2)), ((6, 4), (5, 3)))
+AT_ONCE = ((), (0,), (0, 1), (0, 1, 2), (0, 1, 2, 3, 5, 6), (0, 1, 2, 3, 4, 6, 7), (0, 1, 2, 3, 4, 5, 7), (0, 1, 2, 3, 5, 6))
+THROUGH = ((), (), (), (), ((5, 7),), (), (), ((6, 4),))
 ANSWER = (
     ((1, (1,)), (2, (2,)), (7, (7, 6, 5)), (6, (4,)), (3, (3,))),
     ((2, (2,)), (3, (3,)), (7, (7, 6, 5)), (6, (4,))),
@@ -96,6 +96,17 @@
     def greet(gx, gy):
         pl.semaphore_signal(barrier, inc=1, device_id={"gx": gx, "gy": gy}, device_id_type=MESH)
 
+    def far(table, act):
+        for q in range(8):
+            if table[q]:
+
+                @pl.when(iq == q)
+                def _():
+                    for item in table[q]:
+                        act(item)
+
+    far([[r for r in range(8) if q in AT_ONCE[r]] for q in range(8)], lambda r: greet(r * 4 + im, iy))
+
     for t in range(16):
 
         @pl.when(t != iy)
@@ -119,17 +130,6 @@
         @pl.when(m != im)
         def _():
             greet(iq * 4 + m, iy)
-
-    def far(table, act):
-        for q in range(8):
-            if table[q]:
-
-                @pl.when(iq == q)
-                def _():
-                    for item in table[q]:
-                        act(item)
-
-    far([[r for r in range(8) if q in AT_ONCE[r]] for q in range(8)], lambda r: greet(r * 4 + im, iy))
 
     local = [
         pltpu.make_async_copy(alpha_h, al.at[iy], lsem.at[0]),
@@ -213,8 +213,8 @@
     local[0].wait()
     local[1].wait()
     pl.semaphore_wait(barrier, expected)
+    far(AT_ONCE, lambda q: obs_out(q).start())
     strip(lambda t: alpha_out(t).start())
-    far(AT_ONCE, lambda q: obs_out(q).start())
 
     def halo_copy(ref, d, width, sends, receives):
         dx, dy = DIRS[d]
@@ -417,7 +417,11 @@
         for step in range(STEPS):
             both = found[step * 128 : (step + 1) * 128]
             vo[m, step : step + 1] = jnp.sum(jnp.where(at_gate, both, 0.0), axis=0, keepdims=True)
-    among(4, not_m, lambda m: value_out(m).start())
+
+        @pl.when(m != im)
+        def _():
+            value_out(m).start()
+
 
     each(state_copy, wait_recv, True)
 

time: 43.5 us -> 42.5 us (0.977)
  the two profiles are of different devices: /device:TPU:121 before, /device:TPU:481 now
where the time goes in v5:
time: 42.5 us; the launch traced here: 42.4 us
  Pallas kernels  40.4 us (95%)
  local copies, waits for them, and re-layouts  1.39 us (3%)
  between operations  0.64 us (2%)
    pallas_call x1, Pallas kernels, on_device(): pl.pallas_call(kernel, out_shape=(vm((4, 16, 16, 128), f32), vm((4, 4, 12...  40.4 us
    unnamed x2, local copies, waits for them, and re-layouts  1.39 us

profile of v5, /device:TPU:481, one launch (start us, length us, event | category | flops | bytes accessed | tf_op | source)
XLA Modules:
  0.0 42.4 jit_solution(6807528934935473282)
XLA Ops:
  0.6 40.4 %shard_map.131 = (f32[4,16,16,128]{3,2,1,0:T(8,128)S(1)}, f32[4,4,128]{2,1,0:T(4,128)S(1)}) custom-call(f32[4,16,16,128]{3,2,1,0:T(8,128)} %delta_h.1, f32[16,128]{1,0:T(8,128)} %bitcast.12, f32[16,16,128]{2,1,0:T(8,128)} %eddy_h.1, f32[2,16,16,128]{3,2,1,0:T(8,128)} %courant_h.1, s32[16,16]{1,0:T(8,128)} %tmap_h.1, f32[3,8,128]{2,1,0:T(8,128)} %bitcast.11, ...), custom_call_target="tpu_custom_call" | custom-call | tf_op jit(solution)/shard_map/pallas_call | solution.py:569
  41.0 0.8 %copy.16 = f32[4,16,16,128]{3,2,1,0:T(8,128)} copy(f32[4,16,16,128]{3,2,1,0:T(8,128)S(1)} %get-tuple-element.6) | data formatting | bytes 1048576
  41.8 0.6 %copy.17 = f32[1,4,4,128]{3,2,1,0:T(4,128)} copy(f32[1,4,4,128]{3,2,1,0:T(4,128)S(1)} %bitcast.9) | data formatting | bytes 16384

commit v6 on v5

--- a/solution.py
+++ b/solution.py
@@ -398,7 +398,7 @@
         k5[4, x] = e + half_y
         return carry
 
-    lax.fori_loop(0, XB, derive, 0)
+    lax.fori_loop(0, XB, derive, 0, unroll=True)
 
     far([ANSWER[q] if q < 2 else () for q in range(8)], answer)
     among(4, not_m, lambda m: index_in(m).wait_recv())
@@ -439,7 +439,7 @@
             )
             return carry
 
-        lax.fori_loop(X0 - margin, X1 + margin, body, 0)
+        lax.fori_loop(X0 - margin, X1 + margin, body, 0, unroll=True)
 
     def backward(src, dst, first, last, extra):
         y0, rows = 4, 24
@@ -457,7 +457,7 @@
             )
             return carry
 
-        lax.fori_loop(first, last, body, 0)
+        lax.fori_loop(first, last, body, 0, unroll=True)
         if extra is not None:
             for c in range(4):
                 dst[c, X0:X1, Y0:Y1] += extra[c]

time: 42.5 us -> 42.1 us (level)
  Pallas kernels: 40.4 us -> 39.9 us
    pallas_call x1, Pallas kernels: 40.4 us -> 39.9 us  [on_device(): pl.pallas_call(kernel, out_shape=(vm((4, 16, 16, 128), f32), vm((4, 4, 12...]
where the time goes in v6:
time: 42.1 us; the launch traced here: 41.9 us
  Pallas kernels  39.9 us (95%)
  local copies, waits for them, and re-layouts  1.39 us (3%)
  between operations  0.64 us (2%)
    pallas_call x1, Pallas kernels, on_device(): pl.pallas_call(kernel, out_shape=(vm((4, 16, 16, 128), f32), vm((4, 4, 12...  39.9 us
    unnamed x2, local copies, waits for them, and re-layouts  1.39 us

profile of v6, /device:TPU:481, one launch (start us, length us, event | category | flops | bytes accessed | tf_op | source)
XLA Modules:
  0.0 41.9 jit_solution(14243122630909710622)
XLA Ops:
  0.6 39.9 %shard_map.131 = (f32[4,16,16,128]{3,2,1,0:T(8,128)S(1)}, f32[4,4,128]{2,1,0:T(4,128)S(1)}) custom-call(f32[4,16,16,128]{3,2,1,0:T(8,128)} %delta_h.1, f32[16,128]{1,0:T(8,128)} %bitcast.12, f32[16,16,128]{2,1,0:T(8,128)} %eddy_h.1, f32[2,16,16,128]{3,2,1,0:T(8,128)} %courant_h.1, s32[16,16]{1,0:T(8,128)} %tmap_h.1, f32[3,8,128]{2,1,0:T(8,128)} %bitcast.11, ...), custom_call_target="tpu_custom_call" | custom-call | tf_op jit(solution)/shard_map/pallas_call | solution.py:569
  40.5 0.8 %copy.16 = f32[4,16,16,128]{3,2,1,0:T(8,128)} copy(f32[4,16,16,128]{3,2,1,0:T(8,128)S(1)} %get-tuple-element.6) | data formatting | bytes 1048576
  41.3 0.6 %copy.17 = f32[1,4,4,128]{3,2,1,0:T(4,128)} copy(f32[1,4,4,128]{3,2,1,0:T(4,128)S(1)} %bitcast.9) | data formatting | bytes 16384

commit v7 on v6

--- a/solution.py
+++ b/solution.py
@@ -46,13 +46,13 @@
     return jnp.dot(a, b, preferred_element_type=f32)
 
 
-AT_ONCE = ((), (0,), (0, 1), (0, 1, 2), (0, 1, 2, 3, 5, 6), (0, 1, 2, 3, 4, 6, 7), (0, 1, 2, 3, 4, 5, 7), (0, 1, 2, 3, 5, 6))
-THROUGH = ((), (), (), (), ((5, 7),), (), (), ((6, 4),))
+AT_ONCE = ((), (0,), (0, 1), (0, 1, 2), (0, 1, 2, 3, 5, 6, 7), (0, 1, 2, 3, 4, 6, 7), (0, 1, 2, 3, 4, 5, 7), (0, 1, 2, 3, 5, 6))
+THROUGH = ((), (), (), (), (), (), (), ((6, 4),))
 ANSWER = (
     ((1, (1,)), (2, (2,)), (7, (7, 6, 5)), (6, (4,)), (3, (3,))),
     ((2, (2,)), (3, (3,)), (7, (7, 6, 5)), (6, (4,))),
-    ((3, (3,)), (4, (4, 5, 6)), (5, (7,))),
-    ((4, (4, 6)), (5, (5, 7))),
+    ((3, (3,)), (4, (4, 5, 6, 7))),
+    ((4, (4, 5, 6, 7)),),
     (), (), (), (),
 )
 
@@ -527,12 +527,19 @@
     each(push_copy, wait_recv, True)
     total = None
     for c in range(4):
-        v3[c, X0:X1, Y0:Y1] = v1[c, X0:X1, Y0:Y1] + ry[c]
-        v3[c, X0 : X0 + 3, Y0:Y1] += rx[c, 0:3]
-        v3[c, X1 - 3 : X1, Y0:Y1] += rx[c, 3:6]
-        v3[c, X0 : X0 + 2, Y0:Y1] += rc[c, 0:2]
-        v3[c, X1 - 2 : X1, Y0:Y1] += rc[c, 2:4]
-        high, low = split(v3[c, X0:X1, Y0:Y1].reshape(256, 128))
+        own = v1[c, X0:X1, Y0:Y1] + ry[c]
+        whole = jnp.concatenate(
+            [
+                own[0:2] + rx[c, 0:2] + rc[c, 0:2],
+                own[2:3] + rx[c, 2:3],
+                own[3:13],
+                own[13:14] + rx[c, 3:4],
+                own[14:16] + rx[c, 4:6] + rc[c, 2:4],
+            ],
+            axis=0,
+        )
+        v3[c, X0:X1, Y0:Y1] = whole
+        high, low = split(whole.reshape(256, 128))
         product = dot(selt[:, c * 256 : (c + 1) * 256], jnp.concatenate([high, low], axis=1))
         term = product[:, :128] + product[:, 128:]
         total = term if total is None else total + term

time: 42.1 us -> 42.7 us (1.014); the launches traced: 41.9 us -> 42 us
  no operation moved by 1% of the time
where the time goes in v7:
time: 42.7 us; the launch traced here: 42 us
  Pallas kernels  40 us (94%)
  local copies, waits for them, and re-layouts  1.39 us (3%)
  between operations  0.64 us (1%)
    pallas_call x1, Pallas kernels, on_device(): pl.pallas_call(kernel, out_shape=(vm((4, 16, 16, 128), f32), vm((4, 4, 12...  40 us
    unnamed x2, local copies, waits for them, and re-layouts  1.39 us

profile of v7, /device:TPU:481, one launch (start us, length us, event | category | flops | bytes accessed | tf_op | source)
XLA Modules:
  0.0 42.0 jit_solution(5713870340755339149)
XLA Ops:
  0.6 40.0 %shard_map.131 = (f32[4,16,16,128]{3,2,1,0:T(8,128)S(1)}, f32[4,4,128]{2,1,0:T(4,128)S(1)}) custom-call(f32[4,16,16,128]{3,2,1,0:T(8,128)} %delta_h.1, f32[16,128]{1,0:T(8,128)} %bitcast.12, f32[16,16,128]{2,1,0:T(8,128)} %eddy_h.1, f32[2,16,16,128]{3,2,1,0:T(8,128)} %courant_h.1, s32[16,16]{1,0:T(8,128)} %tmap_h.1, f32[3,8,128]{2,1,0:T(8,128)} %bitcast.11, ...), custom_call_target="tpu_custom_call" | custom-call | tf_op jit(solution)/shard_map/pallas_call | solution.py:576
  40.6 0.8 %copy.16 = f32[4,16,16,128]{3,2,1,0:T(8,128)} copy(f32[4,16,16,128]{3,2,1,0:T(8,128)S(1)} %get-tuple-element.6) | data formatting | bytes 1048576
  41.4 0.6 %copy.17 = f32[1,4,4,128]{3,2,1,0:T(4,128)} copy(f32[1,4,4,128]{3,2,1,0:T(4,128)S(1)} %bitcast.9) | data formatting | bytes 16384
